TPU v7x, 256 devices: a whole 4x4x8 slice. The times are simulated.
256 devices in a mesh: seq: 64 (over x_hi, z, y), head: 4 (over x_lo, core).
Axes of the slice: x: 4 (x_hi: 2, x_lo: 2; x = x_hi * 2 + x_lo), y: 4, z: 8, core: 2. Of those that a mesh axis runs over, the one named last changes fastest.
Arguments:
- queries: bfloat16 [8192, 3584], P('seq', 'head'), may hold values from -256 to 256
- key_codes: bfloat16 [8192, 512], P('seq', 'head'), may hold values from -4 to 4
- value_codes: bfloat16 [8192, 512], P('seq', 'head'), may hold values from -4 to 4
- kv_scales: float32 [2, 64, 4], P(None, 'seq', 'head'), may hold values from 0.5 to 2
- out_weight: bfloat16 [3584, 3584], P('head'), may hold values from -0.09375 to 0.09375
- turn_ids: int32 [8192], replicated, may hold values from 0 to 63, never falling along the last dimension, each value on 1 to 256 neighbouring positions
- block_mask: int32 [64, 64], P('seq'), may hold values 0 or 1
- doc_lengths: int32 [4], replicated, may hold values from 1 to 4096, 8192 in all
Outputs:
- projected: bfloat16 [8192, 3584], P('seq', 'head')
All inputs are finite; a program needn't handle non-finite values. No bound on the sum of `block_mask` on one device may be relied on, other than what follows from the above.
Results may differ from a plain program's by a relative error of at most 0.012.
Values may be sent and summed in bfloat16 or wider, within the bound.
A program may use at most 128 MiB of HBM per device.

v0:
```python
import math

import jax
import jax.numpy as jnp
from jax import lax
from jax.sharding import PartitionSpec as P

HEAD_DIM = 128
BLOCK = 128


masked_score = -1e30


def from_behind(shard, axis, by):
    size = lax.axis_size(axis)
    pairs = [(i, i + by) for i in range(size) if 0 <= i + by < size]
    return lax.ppermute(shard, axis, pairs)


def document_of(places, doc_lengths):
    ends = jnp.cumsum(doc_lengths)
    return jnp.sum((places[:, None] >= ends[None, :]).astype(jnp.int32), axis=1)


def dequantize(codes, scales):
    blocks = scales.shape[0]
    shaped = codes.astype(jnp.float32).reshape(blocks, -1, codes.shape[1])
    return (shaped * scales[:, None, None]).reshape(codes.shape).astype(jnp.bfloat16)


def on_device(
    queries, key_codes, value_codes, kv_scales, out_weight, turn_ids, block_mask, doc_lengths
):
    row_count = queries.shape[0]
    groups = queries.shape[1] // HEAD_DIM
    seq_count = lax.axis_size("seq")
    mine = lax.axis_index("seq")
    scaling = 1.0 / math.sqrt(HEAD_DIM)
    keys = dequantize(key_codes, kv_scales[0, :, 0])
    values = dequantize(value_codes, kv_scales[1, :, 0])
    key_value = jnp.stack([keys, values])
    query_heads = queries.reshape(row_count, groups, HEAD_DIM)
    offsets = jnp.arange(row_count, dtype=jnp.int32)
    query_places = mine * row_count + offsets
    query_turns = lax.dynamic_slice_in_dim(turn_ids, mine * row_count, row_count)
    query_docs = document_of(query_places, doc_lengths)
    mask_rows = block_mask[offsets // BLOCK]

    def attend(state, pair, start):
        width = pair.shape[1]
        key_places = start + jnp.arange(width, dtype=jnp.int32)
        key_turns = lax.dynamic_slice_in_dim(turn_ids, start, width)
        key_docs = document_of(key_places, doc_lengths)
        kept = jnp.take(mask_rows, key_places // BLOCK, axis=1) > 0
        same_block = (query_places // BLOCK)[:, None] == (key_places // BLOCK)[None, :]
        allowed = (
            (key_places[None, :] <= query_places[:, None])
            & (query_docs[:, None] == key_docs[None, :])
            & ((query_turns[:, None] == key_turns[None, :]) | kept | same_block)
        )
        best, totals, summed = state
        scores = (
            jnp.einsum("qgd,kd->gqk", query_heads, pair[0], preferred_element_type=jnp.float32)
            * scaling
        )
        scores = jnp.where(allowed[None], scores, masked_score)
        newest = jnp.maximum(best, jnp.max(scores, axis=2))
        factor = jnp.exp(best - newest)
        weights = jnp.where(allowed[None], jnp.exp(scores - newest[:, :, None]), 0.0)
        totals = totals * factor + jnp.sum(weights, axis=2)
        summed = summed * factor[:, :, None] + jnp.einsum(
            "gqk,kd->gqd", weights.astype(jnp.bfloat16), pair[1], preferred_element_type=jnp.float32
        )
        return (newest, totals, summed)

    initial = (
        jnp.full((groups, row_count), masked_score, jnp.float32),
        jnp.zeros((groups, row_count), jnp.float32),
        jnp.zeros((groups, row_count, HEAD_DIM), jnp.float32),
    )
    state = attend(initial, key_value, mine * row_count)

    def advance(step, carry):
        pair, inner = carry
        pair = from_behind(pair, "seq", 1)
        source = (mine - step) % seq_count
        return (pair, attend(inner, pair, source * row_count))

    count = seq_count - 1
    pair, state = lax.fori_loop(1, count + 1, advance, (key_value, state))
    best, totals, summed = state
    attended = (summed / totals[:, :, None]).astype(jnp.bfloat16)
    weight_heads = out_weight.reshape(groups, HEAD_DIM, out_weight.shape[1])
    partial_value = jnp.einsum(
        "gqd,gde->qe", attended, weight_heads, preferred_element_type=jnp.float32
    )
    return lax.psum_scatter(
        partial_value.astype(jnp.bfloat16), "head", scatter_dimension=1, tiled=True
    )


def solution(mesh):
    placed = (
        P("seq", "head"),
        P("seq", "head"),
        P("seq", "head"),
        P(None, "seq", "head"),
        P("head", None),
        P(),
        P("seq", None),
        P(),
    )
    return jax.shard_map(
        on_device, mesh=mesh, in_specs=placed, out_specs=P("seq", "head"), check_vma=False
    )
```

profile of v0, /device:TPU:4, one launch (start us, length us, event | category | flops | bytes accessed | tf_op | source)
XLA Modules:
  0.0 850.2 jit_solution(15821448232389607410)
XLA Ops:
  18.0 802.0 %while.24 = (s32[]{:T(128)}, bf16[2,128,128]{2,1,0:T(8,128)(2,1)S(1)}, f32[7,128]{1,0:T(8,128)S(1)}, f32[7,128]{1,0:T(8,128)S(1)}, f32[7,128,128]{2,1,0:T(8,128)...) while((s32[]{:T(128)}, ...), condition=%wide.region_8.10_spmd.clone.clone, body=%wide.region_4.9_spmd.clone.clone.sunk | while | flops 60159376 | bytes 3349920 | solution.py:91
  35.6 7.5 collective-permute-done
  73.7 7.5 collective-permute-done
  99.1 7.5 collective-permute-done
  137.2 7.9 collective-permute-done
  264.5 7.9 collective-permute-done
  328.3 7.5 collective-permute-done
  341.0 7.5 collective-permute-done
  353.7 7.5 collective-permute-done
  366.4 7.5 collective-permute-done
  379.1 7.5 collective-permute-done
  391.8 7.9 collective-permute-done
  404.9 7.5 collective-permute-done
  417.6 7.5 collective-permute-done
  519.1 7.8 collective-permute-done
  646.4 7.8 collective-permute-done
  735.6 7.5 collective-permute-done
  748.3 7.5 collective-permute-done
  761.0 7.5 collective-permute-done
  773.7 7.5 collective-permute-done
  786.4 7.5 collective-permute-done
  799.1 7.5 collective-permute-done
  811.8 7.5 collective-permute-done
  825.3 16.2 %reduce-scatter.4.cloned.1.call-done = bf16[896,128]{1,0:T(8,128)(2,1)} async-done(((bf16[3584,128]{1,0:T(8,128)(2,1)}), bf16[896,128]{1,0:T(8,128)(2,1)}) %reduce-scatter.4.cloned.1.call-update) | async-done | bytes 229392
  (1200 shorter events, 645.7 us)
Async XLA Ops:
  6.5 835.1 %reduce-scatter.4.cloned.1.call-start = ((), (), s32[]{:S(2)}) async-start(), calls=%async_computation.1 | async-start | bytes 1146880
  18.0 12.4 %collective-permute-start = (bf16[2,128,128]{2,1,0:T(8,128)(2,1)S(1)}, bf16[2,128,128]{2,1,0:T(8,128)(2,1)S(1)}, u32[]{:S(2)}, u32[]{:S(2)}) collective-permute-start(bf16[2,128,128]{2,1,0:T(8,128)(2,1)S(1)} %get-tuple-element.649), channel_id=1, source_target_pairs={{0,4},{4,8},{8,12},{12,16},{16,20},{20,24},{24,28},{28,32},{32,36}... | collective-permute-start | bytes 196616 | tf_op jit(solution)/shard_map/while/body/eval_jaxpr/ppermute | solution.py:18
  31.2 11.9 %collective-permute-start = (bf16[2,128,128]{2,1,0:T(8,128)(2,1)S(1)}, bf16[2,128,128]{2,1,0:T(8,128)(2,1)S(1)}, u32[]{:S(2)}, u32[]{:S(2)}) collective-permute-start(bf16[2,128,128]{2,1,0:T(8,128)(2,1)S(1)} %get-tuple-element.649), channel_id=1, source_target_pairs={{0,4},{4,8},{8,12},{12,16},{16,20},{20,24},{24,28},{28,32},{32,36}... | collective-permute-start | bytes 196616 | tf_op jit(solution)/shard_map/while/body/eval_jaxpr/ppermute | solution.py:18
  56.6 11.9 %collective-permute-start = (bf16[2,128,128]{2,1,0:T(8,128)(2,1)S(1)}, bf16[2,128,128]{2,1,0:T(8,128)(2,1)S(1)}, u32[]{:S(2)}, u32[]{:S(2)}) collective-permute-start(bf16[2,128,128]{2,1,0:T(8,128)(2,1)S(1)} %get-tuple-element.649), channel_id=1, source_target_pairs={{0,4},{4,8},{8,12},{12,16},{16,20},{20,24},{24,28},{28,32},{32,36}... | collective-permute-start | bytes 196616 | tf_op jit(solution)/shard_map/while/body/eval_jaxpr/ppermute | solution.py:18
  69.3 11.9 %collective-permute-start = (bf16[2,128,128]{2,1,0:T(8,128)(2,1)S(1)}, bf16[2,128,128]{2,1,0:T(8,128)(2,1)S(1)}, u32[]{:S(2)}, u32[]{:S(2)}) collective-permute-start(bf16[2,128,128]{2,1,0:T(8,128)(2,1)S(1)} %get-tuple-element.649), channel_id=1, source_target_pairs={{0,4},{4,8},{8,12},{12,16},{16,20},{20,24},{24,28},{28,32},{32,36}... | collective-permute-start | bytes 196616 | tf_op jit(solution)/shard_map/while/body/eval_jaxpr/ppermute | solution.py:18
  94.7 11.9 %collective-permute-start = (bf16[2,128,128]{2,1,0:T(8,128)(2,1)S(1)}, bf16[2,128,128]{2,1,0:T(8,128)(2,1)S(1)}, u32[]{:S(2)}, u32[]{:S(2)}) collective-permute-start(bf16[2,128,128]{2,1,0:T(8,128)(2,1)S(1)} %get-tuple-element.649), channel_id=1, source_target_pairs={{0,4},{4,8},{8,12},{12,16},{16,20},{20,24},{24,28},{28,32},{32,36}... | collective-permute-start | bytes 196616 | tf_op jit(solution)/shard_map/while/body/eval_jaxpr/ppermute | solution.py:18
  107.4 11.9 %collective-permute-start = (bf16[2,128,128]{2,1,0:T(8,128)(2,1)S(1)}, bf16[2,128,128]{2,1,0:T(8,128)(2,1)S(1)}, u32[]{:S(2)}, u32[]{:S(2)}) collective-permute-start(bf16[2,128,128]{2,1,0:T(8,128)(2,1)S(1)} %get-tuple-element.649), channel_id=1, source_target_pairs={{0,4},{4,8},{8,12},{12,16},{16,20},{20,24},{24,28},{28,32},{32,36}... | collective-permute-start | bytes 196616 | tf_op jit(solution)/shard_map/while/body/eval_jaxpr/ppermute | solution.py:18
  132.7 12.3 %collective-permute-start = (bf16[2,128,128]{2,1,0:T(8,128)(2,1)S(1)}, bf16[2,128,128]{2,1,0:T(8,128)(2,1)S(1)}, u32[]{:S(2)}, u32[]{:S(2)}) collective-permute-start(bf16[2,128,128]{2,1,0:T(8,128)(2,1)S(1)} %get-tuple-element.649), channel_id=1, source_target_pairs={{0,4},{4,8},{8,12},{12,16},{16,20},{20,24},{24,28},{28,32},{32,36}... | collective-permute-start | bytes 196616 | tf_op jit(solution)/shard_map/while/body/eval_jaxpr/ppermute | solution.py:18
  158.5 11.9 %collective-permute-start = (bf16[2,128,128]{2,1,0:T(8,128)(2,1)S(1)}, bf16[2,128,128]{2,1,0:T(8,128)(2,1)S(1)}, u32[]{:S(2)}, u32[]{:S(2)}) collective-permute-start(bf16[2,128,128]{2,1,0:T(8,128)(2,1)S(1)} %get-tuple-element.649), channel_id=1, source_target_pairs={{0,4},{4,8},{8,12},{12,16},{16,20},{20,24},{24,28},{28,32},{32,36}... | collective-permute-start | bytes 196616 | tf_op jit(solution)/shard_map/while/body/eval_jaxpr/ppermute | solution.py:18
  183.9 11.9 %collective-permute-start = (bf16[2,128,128]{2,1,0:T(8,128)(2,1)S(1)}, bf16[2,128,128]{2,1,0:T(8,128)(2,1)S(1)}, u32[]{:S(2)}, u32[]{:S(2)}) collective-permute-start(bf16[2,128,128]{2,1,0:T(8,128)(2,1)S(1)} %get-tuple-element.649), channel_id=1, source_target_pairs={{0,4},{4,8},{8,12},{12,16},{16,20},{20,24},{24,28},{28,32},{32,36}... | collective-permute-start | bytes 196616 | tf_op jit(solution)/shard_map/while/body/eval_jaxpr/ppermute | solution.py:18
  196.6 11.9 %collective-permute-start = (bf16[2,128,128]{2,1,0:T(8,128)(2,1)S(1)}, bf16[2,128,128]{2,1,0:T(8,128)(2,1)S(1)}, u32[]{:S(2)}, u32[]{:S(2)}) collective-permute-start(bf16[2,128,128]{2,1,0:T(8,128)(2,1)S(1)} %get-tuple-element.649), channel_id=1, source_target_pairs={{0,4},{4,8},{8,12},{12,16},{16,20},{20,24},{24,28},{28,32},{32,36}... | collective-permute-start | bytes 196616 | tf_op jit(solution)/shard_map/while/body/eval_jaxpr/ppermute | solution.py:18
  222.0 11.9 %collective-permute-start = (bf16[2,128,128]{2,1,0:T(8,128)(2,1)S(1)}, bf16[2,128,128]{2,1,0:T(8,128)(2,1)S(1)}, u32[]{:S(2)}, u32[]{:S(2)}) collective-permute-start(bf16[2,128,128]{2,1,0:T(8,128)(2,1)S(1)} %get-tuple-element.649), channel_id=1, source_target_pairs={{0,4},{4,8},{8,12},{12,16},{16,20},{20,24},{24,28},{28,32},{32,36}... | collective-permute-start | bytes 196616 | tf_op jit(solution)/shard_map/while/body/eval_jaxpr/ppermute | solution.py:18
  234.7 11.9 %collective-permute-start = (bf16[2,128,128]{2,1,0:T(8,128)(2,1)S(1)}, bf16[2,128,128]{2,1,0:T(8,128)(2,1)S(1)}, u32[]{:S(2)}, u32[]{:S(2)}) collective-permute-start(bf16[2,128,128]{2,1,0:T(8,128)(2,1)S(1)} %get-tuple-element.649), channel_id=1, source_target_pairs={{0,4},{4,8},{8,12},{12,16},{16,20},{20,24},{24,28},{28,32},{32,36}... | collective-permute-start | bytes 196616 | tf_op jit(solution)/shard_map/while/body/eval_jaxpr/ppermute | solution.py:18
  260.1 12.3 %collective-permute-start = (bf16[2,128,128]{2,1,0:T(8,128)(2,1)S(1)}, bf16[2,128,128]{2,1,0:T(8,128)(2,1)S(1)}, u32[]{:S(2)}, u32[]{:S(2)}) collective-permute-start(bf16[2,128,128]{2,1,0:T(8,128)(2,1)S(1)} %get-tuple-element.649), channel_id=1, source_target_pairs={{0,4},{4,8},{8,12},{12,16},{16,20},{20,24},{24,28},{28,32},{32,36}... | collective-permute-start | bytes 196616 | tf_op jit(solution)/shard_map/while/body/eval_jaxpr/ppermute | solution.py:18
  273.1 11.9 %collective-permute-start = (bf16[2,128,128]{2,1,0:T(8,128)(2,1)S(1)}, bf16[2,128,128]{2,1,0:T(8,128)(2,1)S(1)}, u32[]{:S(2)}, u32[]{:S(2)}) collective-permute-start(bf16[2,128,128]{2,1,0:T(8,128)(2,1)S(1)} %get-tuple-element.649), channel_id=1, source_target_pairs={{0,4},{4,8},{8,12},{12,16},{16,20},{20,24},{24,28},{28,32},{32,36}... | collective-permute-start | bytes 196616 | tf_op jit(solution)/shard_map/while/body/eval_jaxpr/ppermute | solution.py:18
  298.5 11.9 %collective-permute-start = (bf16[2,128,128]{2,1,0:T(8,128)(2,1)S(1)}, bf16[2,128,128]{2,1,0:T(8,128)(2,1)S(1)}, u32[]{:S(2)}, u32[]{:S(2)}) collective-permute-start(bf16[2,128,128]{2,1,0:T(8,128)(2,1)S(1)} %get-tuple-element.649), channel_id=1, source_target_pairs={{0,4},{4,8},{8,12},{12,16},{16,20},{20,24},{24,28},{28,32},{32,36}... | collective-permute-start | bytes 196616 | tf_op jit(solution)/shard_map/while/body/eval_jaxpr/ppermute | solution.py:18
  311.2 11.9 %collective-permute-start = (bf16[2,128,128]{2,1,0:T(8,128)(2,1)S(1)}, bf16[2,128,128]{2,1,0:T(8,128)(2,1)S(1)}, u32[]{:S(2)}, u32[]{:S(2)}) collective-permute-start(bf16[2,128,128]{2,1,0:T(8,128)(2,1)S(1)} %get-tuple-element.649), channel_id=1, source_target_pairs={{0,4},{4,8},{8,12},{12,16},{16,20},{20,24},{24,28},{28,32},{32,36}... | collective-permute-start | bytes 196616 | tf_op jit(solution)/shard_map/while/body/eval_jaxpr/ppermute | solution.py:18
  336.6 11.9 %collective-permute-start = (bf16[2,128,128]{2,1,0:T(8,128)(2,1)S(1)}, bf16[2,128,128]{2,1,0:T(8,128)(2,1)S(1)}, u32[]{:S(2)}, u32[]{:S(2)}) collective-permute-start(bf16[2,128,128]{2,1,0:T(8,128)(2,1)S(1)} %get-tuple-element.649), channel_id=1, source_target_pairs={{0,4},{4,8},{8,12},{12,16},{16,20},{20,24},{24,28},{28,32},{32,36}... | collective-permute-start | bytes 196616 | tf_op jit(solution)/shard_map/while/body/eval_jaxpr/ppermute | solution.py:18
  349.3 11.9 %collective-permute-start = (bf16[2,128,128]{2,1,0:T(8,128)(2,1)S(1)}, bf16[2,128,128]{2,1,0:T(8,128)(2,1)S(1)}, u32[]{:S(2)}, u32[]{:S(2)}) collective-permute-start(bf16[2,128,128]{2,1,0:T(8,128)(2,1)S(1)} %get-tuple-element.649), channel_id=1, source_target_pairs={{0,4},{4,8},{8,12},{12,16},{16,20},{20,24},{24,28},{28,32},{32,36}... | collective-permute-start | bytes 196616 | tf_op jit(solution)/shard_map/while/body/eval_jaxpr/ppermute | solution.py:18
  374.7 11.9 %collective-permute-start = (bf16[2,128,128]{2,1,0:T(8,128)(2,1)S(1)}, bf16[2,128,128]{2,1,0:T(8,128)(2,1)S(1)}, u32[]{:S(2)}, u32[]{:S(2)}) collective-permute-start(bf16[2,128,128]{2,1,0:T(8,128)(2,1)S(1)} %get-tuple-element.649), channel_id=1, source_target_pairs={{0,4},{4,8},{8,12},{12,16},{16,20},{20,24},{24,28},{28,32},{32,36}... | collective-permute-start | bytes 196616 | tf_op jit(solution)/shard_map/while/body/eval_jaxpr/ppermute | solution.py:18
  387.4 12.3 %collective-permute-start = (bf16[2,128,128]{2,1,0:T(8,128)(2,1)S(1)}, bf16[2,128,128]{2,1,0:T(8,128)(2,1)S(1)}, u32[]{:S(2)}, u32[]{:S(2)}) collective-permute-start(bf16[2,128,128]{2,1,0:T(8,128)(2,1)S(1)} %get-tuple-element.649), channel_id=1, source_target_pairs={{0,4},{4,8},{8,12},{12,16},{16,20},{20,24},{24,28},{28,32},{32,36}... | collective-permute-start | bytes 196616 | tf_op jit(solution)/shard_map/while/body/eval_jaxpr/ppermute | solution.py:18
  400.5 11.9 %collective-permute-start = (bf16[2,128,128]{2,1,0:T(8,128)(2,1)S(1)}, bf16[2,128,128]{2,1,0:T(8,128)(2,1)S(1)}, u32[]{:S(2)}, u32[]{:S(2)}) collective-permute-start(bf16[2,128,128]{2,1,0:T(8,128)(2,1)S(1)} %get-tuple-element.649), channel_id=1, source_target_pairs={{0,4},{4,8},{8,12},{12,16},{16,20},{20,24},{24,28},{28,32},{32,36}... | collective-permute-start | bytes 196616 | tf_op jit(solution)/shard_map/while/body/eval_jaxpr/ppermute | solution.py:18
  514.7 12.3 %collective-permute-start = (bf16[2,128,128]{2,1,0:T(8,128)(2,1)S(1)}, bf16[2,128,128]{2,1,0:T(8,128)(2,1)S(1)}, u32[]{:S(2)}, u32[]{:S(2)}) collective-permute-start(bf16[2,128,128]{2,1,0:T(8,128)(2,1)S(1)} %get-tuple-element.649), channel_id=1, source_target_pairs={{0,4},{4,8},{8,12},{12,16},{16,20},{20,24},{24,28},{28,32},{32,36}... | collective-permute-start | bytes 196616 | tf_op jit(solution)/shard_map/while/body/eval_jaxpr/ppermute | solution.py:18
  642.0 12.3 %collective-permute-start = (bf16[2,128,128]{2,1,0:T(8,128)(2,1)S(1)}, bf16[2,128,128]{2,1,0:T(8,128)(2,1)S(1)}, u32[]{:S(2)}, u32[]{:S(2)}) collective-permute-start(bf16[2,128,128]{2,1,0:T(8,128)(2,1)S(1)} %get-tuple-element.649), channel_id=1, source_target_pairs={{0,4},{4,8},{8,12},{12,16},{16,20},{20,24},{24,28},{28,32},{32,36}... | collective-permute-start | bytes 196616 | tf_op jit(solution)/shard_map/while/body/eval_jaxpr/ppermute | solution.py:18
  (40 other events, 475.3 us)
Sparse Core Ops, SparseCore 0:
  825.5 16.0 reduce-scatter.3
where the time goes:
time: 859 us; the launch traced here: 850 us
  waiting for transfers between devices  487 us (57%)
  local copies, waits for them, and re-layouts  143 us (17%)
  starting transfers between devices  123 us (14%)
  matrix products  46.8 us (5%)
  other arithmetic  28.5 us (3%)
  between operations  13.5 us (2%)
  loops' own time  8.69 us (1%)
    ppermute x63, waiting for transfers between devices, from_behind(): return lax.ppermute(shard, axis, pairs)  471 us
    ppermute x63, starting transfers between devices, from_behind(): return lax.ppermute(shard, axis, pairs)  123 us
    dynamic_slice x63, local copies, waits for them, and re-layouts, attend(): key_turns = lax.dynamic_slice_in_dim(turn_ids, start, width)  48.1 us
    gather x64, local copies, waits for them, and re-layouts, on_device(): mask_rows = block_mask[offsets // BLOCK]  46.4 us
    gather x64, local copies, waits for them, and re-layouts, attend(): kept = jnp.take(mask_rows, key_places // BLOCK, axis=1) > 0  41.5 us
    dot_general x64, matrix products, attend(): jnp.einsum('gqk,kd->gqd', weights.astype(jnp.bfloat16), pair[1], preferre...  26.5 us
  transfers between devices with their start and end apart: 64, of which 64 were waited for; matrix products, arithmetic and copies ran while one was open for 18% of the time, Pallas kernels for 0%

commit v1 on v0

v1 whole, which is shorter than its diff:
```python
import functools
import math

import jax
import jax.numpy as jnp
from jax import lax
from jax.experimental import pallas as pl
from jax.experimental.pallas import tpu as pltpu
from jax.sharding import PartitionSpec as P

HEAD_DIM = 128
BLOCK = 128
GROUPS = 7
WIDTH = GROUPS * HEAD_DIM
NX, NZ, NY = 2, 8, 4
NHEAD = 4
MASKED = -1e30
FACTOR = math.log2(math.e) / math.sqrt(HEAD_DIM)
MESH = pl.DeviceIdType.MESH
UP, DOWN = 0, 1
COLUMNS = ((0, 256), (256, 256), (512, 256), (768, 128))
CHUNKS = ((0, 512), (512, 384))


def kernel(
    q_ref,
    kc_ref,
    vc_ref,
    scale_ref,
    w_ref,
    turn_ref,
    mask_ref,
    doc_ref,
    out_ref,
    kv,
    qt,
    w,
    bias,
    best,
    totals,
    summed,
    attended,
    rs_out,
    rs_in,
    cross_out,
    cross_in,
    w_sem,
    send_z,
    recv_z,
    send_y,
    recv_y,
    send_relay,
    recv_relay,
    rs_send,
    rs_recv,
    cross_send,
    cross_recv,
):
    seq = lax.axis_index("seq")
    head = lax.axis_index("head")
    xh = seq // (NZ * NY)
    z = (seq // NY) % NZ
    y = seq % NY

    def at(to_xh, to_z, to_y):
        return (to_xh * (NZ * NY) + to_z * NY + to_y, head)

    left = at(xh, z, (y + NY - 1) % NY)
    right = at(xh, z, (y + 1) % NY)
    above = at(xh, (z + 1) % NZ, y)
    below = at(xh, (z + NZ - 1) % NZ, y)
    other = at(1 - xh, z, y)
    chip = head // 2
    core = head % 2
    sibling = (seq, chip * 2 + 1 - core)
    across = (seq, (1 - chip) * 2 + core)

    barrier = pltpu.get_barrier_semaphore()
    partners = (left, right, above, below, other, sibling, across)
    for partner in partners:
        pl.semaphore_signal(barrier, inc=1, device_id=partner, device_id_type=MESH)

    def weight_copy(part):
        return pltpu.make_async_copy(
            w_ref.at[:, pl.ds(part * WIDTH, WIDTH)], w.at[part], w_sem.at[part]
        )

    for part in range(NHEAD):
        weight_copy(part).start()

    kv[UP, z, y, 0] = (kc_ref[...].astype(jnp.float32) * scale_ref[0]).astype(jnp.bfloat16)
    kv[UP, z, y, 1] = jnp.transpose(vc_ref[...].astype(jnp.float32) * scale_ref[1]).astype(
        jnp.bfloat16
    )
    pl.semaphore_wait(barrier, len(partners))

    def z_copy(stream, row, target, slot_row):
        return pltpu.make_async_remote_copy(
            src_ref=kv.at[stream, row, y],
            dst_ref=kv.at[stream, row, y],
            send_sem=send_z.at[stream, slot_row],
            recv_sem=recv_z.at[stream, slot_row],
            device_id=target,
            device_id_type=MESH,
        )

    def x_copy():
        return pltpu.make_async_remote_copy(
            src_ref=kv.at[UP, z, y],
            dst_ref=kv.at[DOWN, z, y],
            send_sem=send_z.at[DOWN, z],
            recv_sem=recv_z.at[DOWN, z],
            device_id=other,
            device_id_type=MESH,
        )

    def y_copy(stream, row, column, target, side):
        return pltpu.make_async_remote_copy(
            src_ref=kv.at[stream, row, column],
            dst_ref=kv.at[stream, row, column],
            send_sem=send_y.at[stream, row, side],
            recv_sem=recv_y.at[stream, row, side],
            device_id=target,
            device_id_type=MESH,
        )

    def relay_copy(stream, row, column, half, target):
        return pltpu.make_async_remote_copy(
            src_ref=kv.at[stream, row, column, half],
            dst_ref=kv.at[stream, row, column, half],
            send_sem=send_relay.at[stream, row, half],
            recv_sem=recv_relay.at[stream, row, half],
            device_id=target,
            device_id_type=MESH,
        )

    y_left = (y + NY - 1) % NY
    y_right = (y + 1) % NY
    y_far = (y + 2) % NY

    @pl.when(xh == 0)
    def _():
        x_copy().start()

    def active(stream, step):
        if stream == UP:
            return (step >= 0) & (step <= z), z - step, above, z < NZ - 1
        return (xh == 1) & (step >= 0) & (step <= NZ - 1 - z), z + step, below, z > 0

    def forward(stream, step):
        on, row, target, more = active(stream, step)

        @pl.when(on)
        def _():
            if stream == UP:

                @pl.when(step > 0)
                def _():
                    z_copy(stream, row, target, row).wait_recv()
            else:
                z_copy(stream, row, target, row).wait_recv()

            @pl.when(more)
            def _():
                z_copy(stream, row, target, row).start()

            y_copy(stream, row, y, right, 0).start()
            y_copy(stream, row, y, left, 1).start()

    def relay(stream, step):
        on, row, _, _ = active(stream, step)

        @pl.when(on)
        def _():
            y_copy(stream, row, y_left, right, 0).wait_recv()
            relay_copy(stream, row, y_left, 0, right).start()
            y_copy(stream, row, y_right, left, 1).wait_recv()
            relay_copy(stream, row, y_right, 1, left).start()

    def drain(stream, step):
        on, row, target, more = active(stream, step)

        @pl.when(on)
        def _():
            @pl.when(more)
            def _():
                z_copy(stream, row, target, row).wait_send()

            y_copy(stream, row, y, right, 0).wait_send()
            y_copy(stream, row, y, left, 1).wait_send()
            relay_copy(stream, row, y_left, 0, right).wait_send()
            relay_copy(stream, row, y_right, 1, left).wait_send()

    lanes = lax.broadcasted_iota(jnp.int32, (1, BLOCK), 1)
    places = seq * BLOCK + lanes
    doc_start = jnp.zeros((1, BLOCK), jnp.int32)
    end = doc_ref[0]
    for index in range(doc_ref.shape[0]):
        doc_start = jnp.where(places >= end, end, doc_start)
        if index + 1 < doc_ref.shape[0]:
            end = end + doc_ref[index + 1]
    own_turns = turn_ref[pl.ds(seq, 1), :]
    earlier = jnp.zeros((1, BLOCK), jnp.int32)
    for back in range(3):
        block = jnp.maximum(seq - back, 0)
        row = turn_ref[pl.ds(block, 1), :].astype(jnp.float32)
        column = jnp.transpose(jnp.broadcast_to(row, (BLOCK, BLOCK))).astype(jnp.int32)
        count = jnp.sum(jnp.where(column < own_turns, 1, 0), axis=0, keepdims=True)
        earlier = earlier + jnp.where(seq >= back, count, 0)
    turn_start = jnp.maximum(seq - 2, 0) * BLOCK + earlier
    key_rows = lax.broadcasted_iota(jnp.int32, (BLOCK, BLOCK), 0)

    for group in range(GROUPS):
        part = slice(group * HEAD_DIM, (group + 1) * HEAD_DIM)
        qt[:, part] = jnp.transpose(q_ref[:, part].astype(jnp.float32)).astype(jnp.bfloat16)
    best[...] = jnp.full_like(best, MASKED)
    totals[...] = jnp.zeros_like(totals)
    summed[...] = jnp.zeros_like(summed)

    def attend(stream, step):
        on, row, _, _ = active(stream, step)

        @pl.when(on)
        def _():
            relay_copy(stream, row, y_far, 0, right).wait_recv()
            relay_copy(stream, row, y_far, 1, left).wait_recv()
            first = row * NY + (xh * (NZ * NY) if stream == UP else 0)
            for column in range(NY):
                block = first + column
                kept = (mask_ref[0, block] == 1) | (block == seq)
                low = jnp.maximum(doc_start, jnp.where(kept, 0, turn_start)) - block * BLOCK
                high = places - block * BLOCK
                allowed = (key_rows >= low) & (key_rows <= high)
                tile = jnp.where(allowed, 0.0, MASKED)
                bias[pl.ds(column * BLOCK, BLOCK), pl.ds(0, BLOCK)] = tile
                bias[pl.ds(column * BLOCK, BLOCK), pl.ds(BLOCK, BLOCK)] = tile
            keys = jnp.concatenate([kv[stream, row, c, 0] for c in range(NY)], axis=0)
            values = jnp.concatenate([kv[stream, row, c, 1] for c in range(NY)], axis=1)
            for start, width in COLUMNS:
                part = pl.ds(start, width)
                scores = (
                    jnp.dot(keys, qt[:, part], preferred_element_type=jnp.float32)
                    + bias[:, pl.ds(0, width)]
                )
                previous = best[:, part]
                newest = jnp.maximum(previous, jnp.max(scores, axis=0, keepdims=True))
                factor = jnp.exp2((previous - newest) * FACTOR)
                weights = jnp.exp2((scores - newest) * FACTOR)
                best[:, part] = newest
                totals[:, part] = totals[:, part] * factor + jnp.sum(
                    weights, axis=0, keepdims=True
                )
                summed[:, part] = summed[:, part] * factor + jnp.dot(
                    values, weights.astype(jnp.bfloat16), preferred_element_type=jnp.float32
                )

    def advance(step, carry):
        forward(UP, step)
        forward(DOWN, step)
        relay(UP, step - 1)
        relay(DOWN, step - 1)
        attend(UP, step - 2)
        attend(DOWN, step - 2)
        return carry

    lax.fori_loop(0, NZ + 2, advance, 0)

    for group in range(GROUPS):
        part = slice(group * HEAD_DIM, (group + 1) * HEAD_DIM)
        attended[:, part] = jnp.transpose(summed[:, part] / totals[:, part]).astype(jnp.bfloat16)
    for part in range(NHEAD):
        weight_copy(part).wait()

    def project(part, start, width):
        return jnp.dot(
            attended[...],
            w[part, :, pl.ds(start, width)],
            preferred_element_type=jnp.float32,
        )

    def sibling_copy(index):
        start, width = CHUNKS[index % 2]
        place = index // 2
        return pltpu.make_async_remote_copy(
            src_ref=rs_out.at[place, :, pl.ds(start, width)],
            dst_ref=rs_in.at[place, :, pl.ds(start, width)],
            send_sem=rs_send.at[index],
            recv_sem=rs_recv.at[index],
            device_id=sibling,
            device_id_type=MESH,
        )

    def cross_copy(index):
        start, width = CHUNKS[index]
        return pltpu.make_async_remote_copy(
            src_ref=cross_out.at[:, pl.ds(start, width)],
            dst_ref=cross_in.at[:, pl.ds(start, width)],
            send_sem=cross_send.at[index],
            recv_sem=cross_recv.at[index],
            device_id=across,
            device_id_type=MESH,
        )

    far = 1 - chip
    for index, (start, width) in enumerate(CHUNKS):
        rs_out[0, :, pl.ds(start, width)] = project(far * 2 + 1 - core, start, width).astype(
            jnp.bfloat16
        )
        sibling_copy(index).start()
    for index, (start, width) in enumerate(CHUNKS):
        mine = project(far * 2 + core, start, width)
        sibling_copy(index).wait_recv()
        cross_out[:, pl.ds(start, width)] = (
            mine + rs_in[0, :, pl.ds(start, width)].astype(jnp.float32)
        ).astype(jnp.bfloat16)
        cross_copy(index).start()
    for index, (start, width) in enumerate(CHUNKS):
        rs_out[1, :, pl.ds(start, width)] = project(chip * 2 + 1 - core, start, width).astype(
            jnp.bfloat16
        )
        sibling_copy(2 + index).start()
    for index, (start, width) in enumerate(CHUNKS):
        mine = project(head, start, width)
        sibling_copy(2 + index).wait_recv()
        mine = mine + rs_in[1, :, pl.ds(start, width)].astype(jnp.float32)
        cross_copy(index).wait_recv()
        out_ref[:, pl.ds(start, width)] = (
            mine + cross_in[:, pl.ds(start, width)].astype(jnp.float32)
        ).astype(jnp.bfloat16)

    for index in range(4):
        sibling_copy(index).wait_send()
    for index in range(2):
        cross_copy(index).wait_send()

    @pl.when(xh == 0)
    def _():
        x_copy().wait_send()

    def finish(step, carry):
        drain(UP, step)
        drain(DOWN, step)
        return carry

    lax.fori_loop(0, NZ, finish, 0)


def on_device(
    queries, key_codes, value_codes, kv_scales, out_weight, turn_ids, block_mask, doc_lengths
):
    vmem = pl.BlockSpec(memory_space=pltpu.VMEM)
    smem = pl.BlockSpec(memory_space=pltpu.SMEM)
    dma = pltpu.SemaphoreType.DMA
    return pl.pallas_call(
        kernel,
        out_shape=jax.ShapeDtypeStruct(queries.shape, jnp.bfloat16),
        in_specs=[
            vmem,
            vmem,
            vmem,
            smem,
            pl.BlockSpec(memory_space=pl.ANY),
            vmem,
            smem,
            smem,
        ],
        out_specs=vmem,
        scratch_shapes=[
            pltpu.VMEM((2, NZ, NY, 2, BLOCK, HEAD_DIM), jnp.bfloat16),
            pltpu.VMEM((HEAD_DIM, WIDTH), jnp.bfloat16),
            pltpu.VMEM((NHEAD, WIDTH, WIDTH), jnp.bfloat16),
            pltpu.VMEM((NY * BLOCK, 2 * BLOCK), jnp.float32),
            pltpu.VMEM((1, WIDTH), jnp.float32),
            pltpu.VMEM((1, WIDTH), jnp.float32),
            pltpu.VMEM((HEAD_DIM, WIDTH), jnp.float32),
            pltpu.VMEM((BLOCK, WIDTH), jnp.bfloat16),
            pltpu.VMEM((2, BLOCK, WIDTH), jnp.bfloat16),
            pltpu.VMEM((2, BLOCK, WIDTH), jnp.bfloat16),
            pltpu.VMEM((BLOCK, WIDTH), jnp.bfloat16),
            pltpu.VMEM((BLOCK, WIDTH), jnp.bfloat16),
            dma((NHEAD,)),
            dma((2, NZ)),
            dma((2, NZ)),
            dma((2, NZ, 2)),
            dma((2, NZ, 2)),
            dma((2, NZ, 2)),
            dma((2, NZ, 2)),
            dma((4,)),
            dma((4,)),
            dma((2,)),
            dma((2,)),
        ],
        compiler_params=pltpu.CompilerParams(
            collective_id=0, has_side_effects=True, vmem_limit_bytes=40 * 1024 * 1024
        ),
    )(
        queries,
        key_codes,
        value_codes,
        kv_scales.reshape(2),
        out_weight,
        turn_ids.reshape(-1, BLOCK),
        block_mask,
        doc_lengths,
    )


def solution(mesh):
    placed = (
        P("seq", "head"),
        P("seq", "head"),
        P("seq", "head"),
        P(None, "seq", "head"),
        P("head", None),
        P(),
        P("seq", None),
        P(),
    )
    return jax.shard_map(
        on_device, mesh=mesh, in_specs=placed, out_specs=P("seq", "head"), check_vma=False
    )
```

time: 859 us -> 65.6 us (0.08)
  waiting for transfers between devices: 487 us -> 0 us
  local copies, waits for them, and re-layouts: 143 us -> 8.69 us
  starting transfers between devices: 123 us -> 0 us
  Pallas kernels: 0 us -> 56.2 us
  matrix products: 46.8 us -> 0 us
  other arithmetic: 28.5 us -> 0 us
  between operations: 13.5 us -> 0.02 us
  loops' own time: 8.69 us -> 0 us
    ppermute x63 -> x0, waiting for transfers between devices: 471 us -> none  [from_behind(): return lax.ppermute(shard, axis, pairs)]
    ppermute x63 -> x0, starting transfers between devices: 123 us -> none  [from_behind(): return lax.ppermute(shard, axis, pairs)]
    gather x128 -> x0, local copies, waits for them, and re-layouts: 87.9 us -> none  [the longest x64 46.4 us: on_device(): mask_rows = block_mask[offsets // BLOCK]]
    pallas_call x0 -> x1, Pallas kernels: none -> 56.2 us  [on_device(): pl.pallas_call(kernel, out_shape=jax.ShapeDtypeStruct(queries.shape, jnp....]
    dynamic_slice x64 -> x0, local copies, waits for them, and re-layouts: 48.9 us -> none  [the longest x63 48.1 us: attend(): key_turns = lax.dynamic_slice_in_dim(turn_ids, start, width)]
    dot_general x129 -> x0, matrix products: 46.8 us -> none  [the longest x64 26.5 us: attend(): jnp.einsum('gqk,kd->gqd', weights.astype(jnp.bfloat16), pair[1], preferre...]
    unnamed x2 -> x0, waiting for transfers between devices: 16.3 us -> none
    reduce_sum x128 -> x0, other arithmetic: 11.4 us -> none  [the longest x64 6.03 us: attend(): totals = totals * factor + jnp.sum(weights, axis=2)]
  transfers between devices with their start and end apart: 64 -> 0, of which waited for: 64 -> 0; matrix products, arithmetic and copies ran while one was open for 18% -> 0% of each run, Pallas kernels for 0% -> 0%
where the time goes in v1:
time: 65.6 us; the launch traced here: 64.9 us
  Pallas kernels  56.2 us (86%)
  local copies, waits for them, and re-layouts  8.69 us (13%)
    pallas_call x1, Pallas kernels, on_device(): pl.pallas_call(kernel, out_shape=jax.ShapeDtypeStruct(queries.shape, jnp....  56.2 us
    unnamed x17, local copies, waits for them, and re-layouts  8.69 us

profile of v1, /device:TPU:4, one launch (start us, length us, event | category | flops | bytes accessed | tf_op | source)
XLA Modules:
  0.0 64.9 jit_solution(14512088289982254796)
XLA Ops:
  0.0 0.0 copy-start
  0.0 2.8 %copy-done = bf16[896,3584]{1,0:T(8,128)(2,1)S(1)} copy-done((bf16[896,3584]{1,0:T(8,128)(2,1)S(1)}, bf16[896,3584]{1,0:T(8,128)(2,1)}, u32[]{:S(2)}) %copy-start) | copy-done | bytes 6422552
  2.8 0.0 copy-start.1
  2.8 0.9 %copy-done.1 = bf16[128,896]{1,0:T(8,128)(2,1)S(1)} copy-done((bf16[128,896]{1,0:T(8,128)(2,1)S(1)}, bf16[128,896]{1,0:T(8,128)(2,1)}, u32[]{:S(2)}) %copy-start.1) | copy-done | bytes 229400
  3.8 0.0 copy-start.2
  3.8 0.8 %copy-done.2 = bf16[128,128]{1,0:T(8,128)(2,1)S(1)} copy-done((bf16[128,128]{1,0:T(8,128)(2,1)S(1)}, bf16[128,128]{1,0:T(8,128)(2,1)}, u32[]{:S(2)}) %copy-start.2) | copy-done | bytes 32792
  4.5 0.0 copy-start.3
  4.5 0.8 %copy-done.3 = bf16[128,128]{1,0:T(8,128)(2,1)S(1)} copy-done((bf16[128,128]{1,0:T(8,128)(2,1)S(1)}, bf16[128,128]{1,0:T(8,128)(2,1)}, u32[]{:S(2)}) %copy-start.3) | copy-done | bytes 32792
  5.3 0.0 copy-start.4
  5.3 0.8 %copy-done.4 = s32[8192]{0:T(1024)S(1)} copy-done((s32[8192]{0:T(1024)S(1)}, s32[8192]{0:T(1024)}, u32[]{:S(2)}) %copy-start.4) | copy-done | bytes 32792
  6.0 0.0 copy-start.5
  6.0 0.7 %copy-done.5 = f32[2,1,1]{0,2,1:T(1,128)S(1)} copy-done((f32[2,1,1]{0,2,1:T(1,128)S(1)}, f32[2,1,1]{0,2,1:T(1,128)}, u32[]{:S(2)}) %copy-start.5) | copy-done | bytes 32
  6.7 0.0 copy-start.6
  6.7 0.7 %copy-done.6 = s32[1,64]{1,0:T(1,128)S(1)} copy-done((s32[1,64]{1,0:T(1,128)S(1)}, s32[1,64]{1,0:T(1,128)}, u32[]{:S(2)}) %copy-start.6) | copy-done | bytes 280
  7.3 0.0 copy-start.7
  7.4 0.7 %copy-done.7 = s32[4]{0:T(128)S(1)} copy-done((s32[4]{0:T(128)S(1)}, s32[4]{0:T(128)}, u32[]{:S(2)}) %copy-start.7) | copy-done | bytes 40
  8.0 56.2 %shard_map.82 = bf16[128,896]{1,0:T(8,128)(2,1)S(1)} custom-call(bf16[128,896]{1,0:T(8,128)(2,1)S(1)} %copy-done.1, bf16[128,128]{1,0:T(8,128)(2,1)S(1)} %copy-done.2, bf16[128,128]{1,0:T(8,128)(2,1)S(1)} %copy-done.3, f32[2]{0:T(128)S(1)} %bitcast.3, bf16[896,3584]{1,0:T(8,128)(2,1)S(1)} %copy-done, s32[64,128]{1,0:T(8,128)S(1)} %bitcast.2, ...), custom_call_target="tpu_custom_call" | custom-call | tf_op jit(solution)/shard_map/pallas_call | solution.py:354
  64.2 0.7 %copy.10 = bf16[128,896]{1,0:T(8,128)(2,1)} copy(bf16[128,896]{1,0:T(8,128)(2,1)S(1)} %shard_map.82) | data formatting | bytes 458752
Async XLA Ops:
  0.0 2.8 %copy-start = (bf16[896,3584]{1,0:T(8,128)(2,1)S(1)}, bf16[896,3584]{1,0:T(8,128)(2,1)}, u32[]{:S(2)}) copy-start(bf16[896,3584]{1,0:T(8,128)(2,1)} %w_ref.1) | copy-start | bytes 19267588
  2.8 0.9 %copy-start.1 = (bf16[128,896]{1,0:T(8,128)(2,1)S(1)}, bf16[128,896]{1,0:T(8,128)(2,1)}, u32[]{:S(2)}) copy-start(bf16[128,896]{1,0:T(8,128)(2,1)} %q_ref.1) | copy-start | bytes 688132
  3.8 0.8 %copy-start.2 = (bf16[128,128]{1,0:T(8,128)(2,1)S(1)}, bf16[128,128]{1,0:T(8,128)(2,1)}, u32[]{:S(2)}) copy-start(bf16[128,128]{1,0:T(8,128)(2,1)} %kc_ref.1) | copy-start | bytes 98308
  4.5 0.8 %copy-start.3 = (bf16[128,128]{1,0:T(8,128)(2,1)S(1)}, bf16[128,128]{1,0:T(8,128)(2,1)}, u32[]{:S(2)}) copy-start(bf16[128,128]{1,0:T(8,128)(2,1)} %vc_ref.1) | copy-start | bytes 98308
  5.3 0.8 %copy-start.4 = (s32[8192]{0:T(1024)S(1)}, s32[8192]{0:T(1024)}, u32[]{:S(2)}) copy-start(s32[8192]{0:T(1024)} %param.13) | copy-start | bytes 98308
  6.0 0.7 %copy-start.5 = (f32[2,1,1]{0,2,1:T(1,128)S(1)}, f32[2,1,1]{0,2,1:T(1,128)}, u32[]{:S(2)}) copy-start(f32[2,1,1]{0,2,1:T(1,128)} %param.11) | copy-start | bytes 28
  6.7 0.7 %copy-start.6 = (s32[1,64]{1,0:T(1,128)S(1)}, s32[1,64]{1,0:T(1,128)}, u32[]{:S(2)}) copy-start(s32[1,64]{1,0:T(1,128)} %mask_ref.1) | copy-start | bytes 772
  7.3 0.7 %copy-start.7 = (s32[4]{0:T(128)S(1)}, s32[4]{0:T(128)}, u32[]{:S(2)}) copy-start(s32[4]{0:T(128)} %doc_ref.1) | copy-start | bytes 52

commit v2 on v1

--- a/solution.py
+++ b/solution.py
@@ -18,20 +18,28 @@
 FACTOR = math.log2(math.e) / math.sqrt(HEAD_DIM)
 MESH = pl.DeviceIdType.MESH
 UP, DOWN = 0, 1
+WINDOW, RELAY_LAG, ATTEND_LAG = 3, 2, 4
 COLUMNS = ((0, 256), (256, 256), (512, 256), (768, 128))
 CHUNKS = ((0, 512), (512, 384))
 
 
 def kernel(
+    q_hbm,
+    kc_hbm,
+    vc_hbm,
+    scale_hbm,
+    w_ref,
+    turn_hbm,
+    mask_hbm,
+    doc_hbm,
+    out_ref,
     q_ref,
     kc_ref,
     vc_ref,
     scale_ref,
-    w_ref,
     turn_ref,
     mask_ref,
     doc_ref,
-    out_ref,
     kv,
     qt,
     w,
@@ -45,6 +53,7 @@
     cross_out,
     cross_in,
     w_sem,
+    in_sem,
     send_z,
     recv_z,
     send_y,
@@ -67,8 +76,6 @@
 
     left = at(xh, z, (y + NY - 1) % NY)
     right = at(xh, z, (y + 1) % NY)
-    above = at(xh, (z + 1) % NZ, y)
-    below = at(xh, (z + NZ - 1) % NZ, y)
     other = at(1 - xh, z, y)
     chip = head // 2
     core = head % 2
@@ -76,7 +83,9 @@
     across = (seq, (1 - chip) * 2 + core)
 
     barrier = pltpu.get_barrier_semaphore()
-    partners = (left, right, above, below, other, sibling, across)
+    partners = [left, right, sibling, across, other]
+    for step in range(1, NZ):
+        partners += [at(xh, (z + step) % NZ, y), at(1 - xh, (z + step) % NZ, y)]
     for partner in partners:
         pl.semaphore_signal(barrier, inc=1, device_id=partner, device_id_type=MESH)
 
@@ -85,8 +94,23 @@
             w_ref.at[:, pl.ds(part * WIDTH, WIDTH)], w.at[part], w_sem.at[part]
         )
 
-    for part in range(NHEAD):
-        weight_copy(part).start()
+    staged = (
+        (kc_hbm, kc_ref),
+        (vc_hbm, vc_ref),
+        (scale_hbm, scale_ref),
+        (doc_hbm, doc_ref),
+        (turn_hbm, turn_ref),
+        (mask_hbm, mask_ref),
+        (q_hbm, q_ref),
+    )
+    stage = [
+        pltpu.make_async_copy(source, target, in_sem.at[index])
+        for index, (source, target) in enumerate(staged)
+    ]
+    for copy in stage:
+        copy.start()
+    for copy in stage[:3]:
+        copy.wait()
 
     kv[UP, z, y, 0] = (kc_ref[...].astype(jnp.float32) * scale_ref[0]).astype(jnp.bfloat16)
     kv[UP, z, y, 1] = jnp.transpose(vc_ref[...].astype(jnp.float32) * scale_ref[1]).astype(
@@ -94,22 +118,32 @@
     )
     pl.semaphore_wait(barrier, len(partners))
 
-    def z_copy(stream, row, target, slot_row):
+    def up_copy(step):
+        return pltpu.make_async_remote_copy(
+            src_ref=kv.at[UP, z, y],
+            dst_ref=kv.at[UP, z, y],
+            send_sem=send_z.at[UP, step],
+            recv_sem=recv_z.at[UP, z],
+            device_id=at(xh, (z + step) % NZ, y),
+            device_id_type=MESH,
+        )
+
+    def down_copy(step):
+        return pltpu.make_async_remote_copy(
+            src_ref=kv.at[UP, z, y],
+            dst_ref=kv.at[DOWN, z, y],
+            send_sem=send_z.at[DOWN, step],
+            recv_sem=recv_z.at[DOWN, z],
+            device_id=at(1 - xh, (z + NZ - step) % NZ, y),
+            device_id_type=MESH,
+        )
+
+    def arrival(stream, row):
         return pltpu.make_async_remote_copy(
             src_ref=kv.at[stream, row, y],
             dst_ref=kv.at[stream, row, y],
-            send_sem=send_z.at[stream, slot_row],
-            recv_sem=recv_z.at[stream, slot_row],
-            device_id=target,
-            device_id_type=MESH,
-        )
-
-    def x_copy():
-        return pltpu.make_async_remote_copy(
-            src_ref=kv.at[UP, z, y],
-            dst_ref=kv.at[DOWN, z, y],
-            send_sem=send_z.at[DOWN, z],
-            recv_sem=recv_z.at[DOWN, z],
+            send_sem=send_z.at[stream, 0],
+            recv_sem=recv_z.at[stream, row],
             device_id=other,
             device_id_type=MESH,
         )
@@ -138,37 +172,41 @@
     y_right = (y + 1) % NY
     y_far = (y + 2) % NY
 
-    @pl.when(xh == 0)
-    def _():
-        x_copy().start()
-
     def active(stream, step):
         if stream == UP:
-            return (step >= 0) & (step <= z), z - step, above, z < NZ - 1
-        return (xh == 1) & (step >= 0) & (step <= NZ - 1 - z), z + step, below, z > 0
+            return (step >= 0) & (step <= z), z - step
+        return (xh == 1) & (step >= 0) & (step <= NZ - 1 - z), z + step
+
+    def column_send(step, act):
+        @pl.when((xh == 0) & (step <= z))
+        def _():
+            act(down_copy(step))
+
+        @pl.when((step > 0) & (z + step < NZ))
+        def _():
+            act(up_copy(step))
 
     def forward(stream, step):
-        on, row, target, more = active(stream, step)
+        on, row = active(stream, step)
+
+        if stream == UP:
+            on = on & (step > 0)
 
         @pl.when(on)
         def _():
-            if stream == UP:
-
-                @pl.when(step > 0)
-                def _():
-                    z_copy(stream, row, target, row).wait_recv()
-            else:
-                z_copy(stream, row, target, row).wait_recv()
-
-            @pl.when(more)
-            def _():
-                z_copy(stream, row, target, row).start()
-
+            arrival(stream, row).wait_recv()
             y_copy(stream, row, y, right, 0).start()
             y_copy(stream, row, y, left, 1).start()
 
+    y_copy(UP, z, y, right, 0).start()
+    y_copy(UP, z, y, left, 1).start()
+    for step in range(WINDOW):
+        column_send(step, lambda copy: copy.start())
+    for part in range(NHEAD):
+        weight_copy(part).start()
+
     def relay(stream, step):
-        on, row, _, _ = active(stream, step)
+        on, row = active(stream, step)
 
         @pl.when(on)
         def _():
@@ -178,18 +216,17 @@
             relay_copy(stream, row, y_right, 1, left).start()
 
     def drain(stream, step):
-        on, row, target, more = active(stream, step)
+        on, row = active(stream, step)
 
         @pl.when(on)
         def _():
-            @pl.when(more)
-            def _():
-                z_copy(stream, row, target, row).wait_send()
-
             y_copy(stream, row, y, right, 0).wait_send()
             y_copy(stream, row, y, left, 1).wait_send()
             relay_copy(stream, row, y_left, 0, right).wait_send()
             relay_copy(stream, row, y_right, 1, left).wait_send()
+
+    for copy in stage[3:]:
+        copy.wait()
 
     lanes = lax.broadcasted_iota(jnp.int32, (1, BLOCK), 1)
     places = seq * BLOCK + lanes
@@ -218,7 +255,7 @@
     summed[...] = jnp.zeros_like(summed)
 
     def attend(stream, step):
-        on, row, _, _ = active(stream, step)
+        on, row = active(stream, step)
 
         @pl.when(on)
         def _():
@@ -255,15 +292,20 @@
                 )
 
     def advance(step, carry):
-        forward(UP, step)
-        forward(DOWN, step)
-        relay(UP, step - 1)
-        relay(DOWN, step - 1)
-        attend(UP, step - 2)
-        attend(DOWN, step - 2)
+        @pl.when(step < NZ)
+        def _():
+            forward(UP, step)
+            forward(DOWN, step)
+            column_send(step, lambda copy: copy.wait_send())
+
+        column_send(step + WINDOW, lambda copy: copy.start())
+        relay(UP, step - RELAY_LAG)
+        relay(DOWN, step - RELAY_LAG)
+        attend(UP, step - ATTEND_LAG)
+        attend(DOWN, step - ATTEND_LAG)
         return carry
 
-    lax.fori_loop(0, NZ + 2, advance, 0)
+    lax.fori_loop(0, NZ + ATTEND_LAG, advance, 0)
 
     for group in range(GROUPS):
         part = slice(group * HEAD_DIM, (group + 1) * HEAD_DIM)
@@ -333,10 +375,6 @@
     for index in range(2):
         cross_copy(index).wait_send()
 
-    @pl.when(xh == 0)
-    def _():
-        x_copy().wait_send()
-
     def finish(step, carry):
         drain(UP, step)
         drain(DOWN, step)
@@ -348,24 +386,20 @@
 def on_device(
     queries, key_codes, value_codes, kv_scales, out_weight, turn_ids, block_mask, doc_lengths
 ):
-    vmem = pl.BlockSpec(memory_space=pltpu.VMEM)
-    smem = pl.BlockSpec(memory_space=pltpu.SMEM)
     dma = pltpu.SemaphoreType.DMA
     return pl.pallas_call(
         kernel,
         out_shape=jax.ShapeDtypeStruct(queries.shape, jnp.bfloat16),
-        in_specs=[
-            vmem,
-            vmem,
-            vmem,
-            smem,
-            pl.BlockSpec(memory_space=pl.ANY),
-            vmem,
-            smem,
-            smem,
-        ],
-        out_specs=vmem,
+        in_specs=[pl.BlockSpec(memory_space=pltpu.HBM)] * 8,
+        out_specs=pl.BlockSpec(memory_space=pltpu.VMEM),
         scratch_shapes=[
+            pltpu.VMEM(queries.shape, jnp.bfloat16),
+            pltpu.VMEM(key_codes.shape, jnp.bfloat16),
+            pltpu.VMEM(value_codes.shape, jnp.bfloat16),
+            pltpu.SMEM((2,), jnp.float32),
+            pltpu.VMEM((turn_ids.shape[0] // BLOCK, BLOCK), jnp.int32),
+            pltpu.SMEM(block_mask.shape, jnp.int32),
+            pltpu.SMEM(doc_lengths.shape, jnp.int32),
             pltpu.VMEM((2, NZ, NY, 2, BLOCK, HEAD_DIM), jnp.bfloat16),
             pltpu.VMEM((HEAD_DIM, WIDTH), jnp.bfloat16),
             pltpu.VMEM((NHEAD, WIDTH, WIDTH), jnp.bfloat16),
@@ -379,6 +413,7 @@
             pltpu.VMEM((BLOCK, WIDTH), jnp.bfloat16),
             pltpu.VMEM((BLOCK, WIDTH), jnp.bfloat16),
             dma((NHEAD,)),
+            dma((7,)),
             dma((2, NZ)),
             dma((2, NZ)),
             dma((2, NZ, 2)),
@@ -394,14 +429,19 @@
             collective_id=0, has_side_effects=True, vmem_limit_bytes=40 * 1024 * 1024
         ),
     )(
-        queries,
-        key_codes,
-        value_codes,
-        kv_scales.reshape(2),
-        out_weight,
-        turn_ids.reshape(-1, BLOCK),
-        block_mask,
-        doc_lengths,
+        *(
+            pltpu.with_memory_space_constraint(operand, pltpu.HBM)
+            for operand in (
+                queries,
+                key_codes,
+                value_codes,
+                kv_scales.reshape(2),
+                out_weight,
+                turn_ids.reshape(-1, BLOCK),
+                block_mask,
+                doc_lengths,
+            )
+        )
     )
 
 

time: 65.6 us -> 52.7 us (0.80)
  the two profiles are of different devices: /device:TPU:4 before, /device:TPU:69 now
where the time goes in v2:
time: 52.7 us; the launch traced here: 52.6 us
  Pallas kernels  51.9 us (98%)
  local copies, waits for them, and re-layouts  0.69 us (1%)
    pallas_call x1, Pallas kernels, on_device(): pl.pallas_call(kernel, out_shape=jax.ShapeDtypeStruct(queries.shape, jnp....  51.9 us

profile of v2, /device:TPU:69, one launch (start us, length us, event | category | flops | bytes accessed | tf_op | source)
XLA Modules:
  0.0 52.6 jit_solution(15536244320866952197)
XLA Ops:
  0.0 51.9 %shard_map.82 = bf16[128,896]{1,0:T(8,128)(2,1)S(1)} custom-call(bf16[128,896]{1,0:T(8,128)(2,1)} %q_hbm.1, bf16[128,128]{1,0:T(8,128)(2,1)} %kc_hbm.1, bf16[128,128]{1,0:T(8,128)(2,1)} %vc_hbm.1, f32[2]{0:T(128)} %bitcast.3, bf16[896,3584]{1,0:T(8,128)(2,1)} %w_ref.1, s32[64,128]{1,0:T(8,128)} %bitcast.2, s32[1,64]{1,0:T(1,128)} %mask_hbm.1, s32[4]{0:T(128)} %doc_hbm.1), custom_call_target="tpu_custom_call" | custom-call | tf_op jit(solution)/shard_map/pallas_call | solution.py:390
  51.9 0.7 %copy.10 = bf16[128,896]{1,0:T(8,128)(2,1)} copy(bf16[128,896]{1,0:T(8,128)(2,1)S(1)} %shard_map.82) | data formatting | bytes 458752

commit v3 on v2

--- a/solution.py
+++ b/solution.py
@@ -19,7 +19,7 @@
 MESH = pl.DeviceIdType.MESH
 UP, DOWN = 0, 1
 WINDOW, RELAY_LAG, ATTEND_LAG = 3, 2, 4
-COLUMNS = ((0, 256), (256, 256), (512, 256), (768, 128))
+HEADS = 2
 CHUNKS = ((0, 512), (512, 384))
 
 
@@ -41,11 +41,11 @@
     mask_ref,
     doc_ref,
     kv,
-    qt,
+    q_rows,
     w,
     bias,
+    starts,
     best,
-    totals,
     summed,
     attended,
     rs_out,
@@ -113,9 +113,7 @@
         copy.wait()
 
     kv[UP, z, y, 0] = (kc_ref[...].astype(jnp.float32) * scale_ref[0]).astype(jnp.bfloat16)
-    kv[UP, z, y, 1] = jnp.transpose(vc_ref[...].astype(jnp.float32) * scale_ref[1]).astype(
-        jnp.bfloat16
-    )
+    kv[UP, z, y, 1] = (vc_ref[...].astype(jnp.float32) * scale_ref[1]).astype(jnp.bfloat16)
     pl.semaphore_wait(barrier, len(partners))
 
     def up_copy(step):
@@ -245,13 +243,20 @@
         count = jnp.sum(jnp.where(column < own_turns, 1, 0), axis=0, keepdims=True)
         earlier = earlier + jnp.where(seq >= back, count, 0)
     turn_start = jnp.maximum(seq - 2, 0) * BLOCK + earlier
-    key_rows = lax.broadcasted_iota(jnp.int32, (BLOCK, BLOCK), 0)
+
+    def along_rows(row):
+        wide = jnp.broadcast_to(row.astype(jnp.float32), (BLOCK, BLOCK))
+        return jnp.transpose(wide).astype(jnp.int32)
+
+    starts[0] = along_rows(doc_start)
+    starts[1] = along_rows(turn_start)
+    key_lanes = lax.broadcasted_iota(jnp.int32, (BLOCK, BLOCK), 1)
+    query_places = seq * BLOCK + lax.broadcasted_iota(jnp.int32, (BLOCK, BLOCK), 0)
 
     for group in range(GROUPS):
-        part = slice(group * HEAD_DIM, (group + 1) * HEAD_DIM)
-        qt[:, part] = jnp.transpose(q_ref[:, part].astype(jnp.float32)).astype(jnp.bfloat16)
+        rows = slice(group * BLOCK, (group + 1) * BLOCK)
+        q_rows[rows, :] = q_ref[:, group * HEAD_DIM : (group + 1) * HEAD_DIM]
     best[...] = jnp.full_like(best, MASKED)
-    totals[...] = jnp.zeros_like(totals)
     summed[...] = jnp.zeros_like(summed)
 
     def attend(stream, step):
@@ -265,30 +270,31 @@
             for column in range(NY):
                 block = first + column
                 kept = (mask_ref[0, block] == 1) | (block == seq)
-                low = jnp.maximum(doc_start, jnp.where(kept, 0, turn_start)) - block * BLOCK
-                high = places - block * BLOCK
-                allowed = (key_rows >= low) & (key_rows <= high)
-                tile = jnp.where(allowed, 0.0, MASKED)
-                bias[pl.ds(column * BLOCK, BLOCK), pl.ds(0, BLOCK)] = tile
-                bias[pl.ds(column * BLOCK, BLOCK), pl.ds(BLOCK, BLOCK)] = tile
+                low = jnp.maximum(starts[0], jnp.where(kept, 0, starts[1]))
+                places = block * BLOCK + key_lanes
+                allowed = (places >= low) & (places <= query_places)
+                bias[:, pl.ds(column * BLOCK, BLOCK)] = jnp.where(allowed, 0.0, MASKED)
             keys = jnp.concatenate([kv[stream, row, c, 0] for c in range(NY)], axis=0)
-            values = jnp.concatenate([kv[stream, row, c, 1] for c in range(NY)], axis=1)
-            for start, width in COLUMNS:
-                part = pl.ds(start, width)
-                scores = (
-                    jnp.dot(keys, qt[:, part], preferred_element_type=jnp.float32)
-                    + bias[:, pl.ds(0, width)]
+            values = jnp.concatenate([kv[stream, row, c, 1] for c in range(NY)], axis=0)
+            values = jnp.concatenate([values, jnp.ones_like(values)], axis=1)
+            for start in range(0, GROUPS, HEADS):
+                heads = min(HEADS, GROUPS - start)
+                rows = pl.ds(start * BLOCK, heads * BLOCK)
+                scores = lax.dot_general(
+                    q_rows[rows, :],
+                    keys,
+                    (((1,), (1,)), ((), ())),
+                    preferred_element_type=jnp.float32,
                 )
-                previous = best[:, part]
-                newest = jnp.maximum(previous, jnp.max(scores, axis=0, keepdims=True))
+                scores = scores.reshape(heads, BLOCK, NY * BLOCK) + bias[...][None]
+                scores = scores.reshape(heads * BLOCK, NY * BLOCK)
+                previous = best[rows, :]
+                newest = jnp.maximum(previous, jnp.max(scores, axis=1, keepdims=True))
                 factor = jnp.exp2((previous - newest) * FACTOR)
                 weights = jnp.exp2((scores - newest) * FACTOR)
-                best[:, part] = newest
-                totals[:, part] = totals[:, part] * factor + jnp.sum(
-                    weights, axis=0, keepdims=True
-                )
-                summed[:, part] = summed[:, part] * factor + jnp.dot(
-                    values, weights.astype(jnp.bfloat16), preferred_element_type=jnp.float32
+                best[rows, :] = newest
+                summed[rows, :] = summed[rows, :] * factor + jnp.dot(
+                    weights.astype(jnp.bfloat16), values, preferred_element_type=jnp.float32
                 )
 
     def advance(step, carry):
@@ -308,8 +314,10 @@
     lax.fori_loop(0, NZ + ATTEND_LAG, advance, 0)
 
     for group in range(GROUPS):
-        part = slice(group * HEAD_DIM, (group + 1) * HEAD_DIM)
-        attended[:, part] = jnp.transpose(summed[:, part] / totals[:, part]).astype(jnp.bfloat16)
+        rows = slice(group * BLOCK, (group + 1) * BLOCK)
+        attended[:, group * HEAD_DIM : (group + 1) * HEAD_DIM] = (
+            summed[rows, :HEAD_DIM] / summed[rows, HEAD_DIM:]
+        ).astype(jnp.bfloat16)
     for part in range(NHEAD):
         weight_copy(part).wait()
 
@@ -401,12 +409,12 @@
             pltpu.SMEM(block_mask.shape, jnp.int32),
             pltpu.SMEM(doc_lengths.shape, jnp.int32),
             pltpu.VMEM((2, NZ, NY, 2, BLOCK, HEAD_DIM), jnp.bfloat16),
-            pltpu.VMEM((HEAD_DIM, WIDTH), jnp.bfloat16),
+            pltpu.VMEM((GROUPS * BLOCK, HEAD_DIM), jnp.bfloat16),
             pltpu.VMEM((NHEAD, WIDTH, WIDTH), jnp.bfloat16),
-            pltpu.VMEM((NY * BLOCK, 2 * BLOCK), jnp.float32),
-            pltpu.VMEM((1, WIDTH), jnp.float32),
-            pltpu.VMEM((1, WIDTH), jnp.float32),
-            pltpu.VMEM((HEAD_DIM, WIDTH), jnp.float32),
+            pltpu.VMEM((BLOCK, NY * BLOCK), jnp.float32),
+            pltpu.VMEM((2, BLOCK, BLOCK), jnp.int32),
+            pltpu.VMEM((GROUPS * BLOCK, 1), jnp.float32),
+            pltpu.VMEM((GROUPS * BLOCK, 2 * HEAD_DIM), jnp.float32),
             pltpu.VMEM((BLOCK, WIDTH), jnp.bfloat16),
             pltpu.VMEM((2, BLOCK, WIDTH), jnp.bfloat16),
             pltpu.VMEM((2, BLOCK, WIDTH), jnp.bfloat16),

time: 52.7 us -> 50.4 us (0.956)
  the two profiles are of different devices: /device:TPU:69 before, /device:TPU:4 now
where the time goes in v3:
time: 50.4 us; the launch traced here: 50.1 us
  Pallas kernels  49.4 us (98%)
  local copies, waits for them, and re-layouts  0.69 us (1%)
    pallas_call x1, Pallas kernels, on_device(): pl.pallas_call(kernel, out_shape=jax.ShapeDtypeStruct(queries.shape, jnp....  49.4 us

profile of v3, /device:TPU:4, one launch (start us, length us, event | category | flops | bytes accessed | tf_op | source)
XLA Modules:
  0.0 50.1 jit_solution(17552760751863488410)
XLA Ops:
  0.0 49.4 %shard_map.82 = bf16[128,896]{1,0:T(8,128)(2,1)S(1)} custom-call(bf16[128,896]{1,0:T(8,128)(2,1)} %q_hbm.1, bf16[128,128]{1,0:T(8,128)(2,1)} %kc_hbm.1, bf16[128,128]{1,0:T(8,128)(2,1)} %vc_hbm.1, f32[2]{0:T(128)} %bitcast.3, bf16[896,3584]{1,0:T(8,128)(2,1)} %w_ref.1, s32[64,128]{1,0:T(8,128)} %bitcast.2, s32[1,64]{1,0:T(1,128)} %mask_hbm.1, s32[4]{0:T(128)} %doc_hbm.1), custom_call_target="tpu_custom_call" | custom-call | tf_op jit(solution)/shard_map/pallas_call | solution.py:398
  49.4 0.7 %copy.10 = bf16[128,896]{1,0:T(8,128)(2,1)} copy(bf16[128,896]{1,0:T(8,128)(2,1)S(1)} %shard_map.82) | data formatting | bytes 458752

commit v4 on v3

v4 whole, which is shorter than its diff:
```python
import math

import jax
import jax.numpy as jnp
from jax import lax
from jax.experimental import pallas as pl
from jax.experimental.pallas import tpu as pltpu
from jax.sharding import PartitionSpec as P

HEAD_DIM = 128
BLOCK = 128
GROUPS = 7
WIDTH = GROUPS * HEAD_DIM
NX, NZ, NY = 2, 8, 4
PAIRS = NZ // 2
NHEAD = 4
MASKED = -1e30
FACTOR = math.log2(math.e) / math.sqrt(HEAD_DIM)
MESH = pl.DeviceIdType.MESH
UP, DOWN = 0, 1
WINDOW, SHARE_LAG, ATTEND_LAG = 2, 1, 2
HEADS = 2
PARTS = -(-GROUPS // HEADS)
CHUNKS = ((0, 512), (512, 384))


def kernel(
    q_hbm,
    kc_hbm,
    vc_hbm,
    scale_hbm,
    w_ref,
    turn_hbm,
    mask_hbm,
    doc_hbm,
    out_ref,
    q_ref,
    kc_ref,
    vc_ref,
    scale_ref,
    turn_ref,
    mask_ref,
    doc_ref,
    own,
    kv,
    q_rows,
    w,
    bias,
    starts,
    best,
    summed,
    result,
    attended,
    rs_out,
    rs_in,
    cross_out,
    cross_in,
    w_sem,
    in_sem,
    send_z,
    recv_z,
    send_y,
    recv_y,
    send_core,
    recv_core,
    swap_send,
    swap_recv,
    rs_send,
    rs_recv,
    cross_send,
    cross_recv,
):
    seq = lax.axis_index("seq")
    head = lax.axis_index("head")
    xh = seq // (NZ * NY)
    z = (seq // NY) % NZ
    y = seq % NY

    chip = head // 2
    core = head % 2
    pair = z // 2
    parity = z % 2
    home = core == parity
    row = pair * 2 + core
    query_seq = xh * (NZ * NY) + row * NY + y

    def at(to_xh, to_z, to_y, to_core):
        return (to_xh * (NZ * NY) + to_z * NY + to_y, chip * 2 + to_core)

    left = at(xh, z, (y + NY - 1) % NY, core)
    right = at(xh, z, (y + 1) % NY, core)
    opposite = at(xh, z, (y + 2) % NY, core)
    sibling = at(xh, z, y, 1 - core)
    partner = at(xh, z + 1 - 2 * parity, y, 1 - core)
    across = (seq, (1 - chip) * 2 + core)

    barrier = pltpu.get_barrier_semaphore()

    def greet(device):
        pl.semaphore_signal(barrier, inc=1, device_id=device, device_id_type=MESH)

    for device in (left, right, opposite, across):
        greet(device)
    for half in range(NX):
        for index in range(PAIRS):
            greet(at(half, 2 * index + 1 - core, y, parity))
            for to_core in range(2):

                @pl.when((half != xh) | (2 * index + core != z) | (to_core != core))
                def _():
                    greet(at(half, 2 * index + core, y, to_core))

    greeted = 4 + 3 * NX * PAIRS - jnp.where(home, 1, 0)

    def weight_copy(part):
        return pltpu.make_async_copy(
            w_ref.at[:, pl.ds(part * WIDTH, WIDTH)], w.at[part], w_sem.at[part]
        )

    staged = (
        (kc_hbm, kc_ref),
        (vc_hbm, vc_ref),
        (scale_hbm, scale_ref),
        (doc_hbm, doc_ref),
        (turn_hbm, turn_ref),
    )
    stage = [
        pltpu.make_async_copy(source, target, in_sem.at[index])
        for index, (source, target) in enumerate(staged)
    ]
    for copy in stage:
        copy.start()
    for copy in stage[:3]:
        copy.wait()

    own[0] = (kc_ref[...].astype(jnp.float32) * scale_ref[0]).astype(jnp.bfloat16)
    own[1] = (vc_ref[...].astype(jnp.float32) * scale_ref[1]).astype(jnp.bfloat16)

    @pl.when(home)
    def _():
        kv[UP, pair, y, core, parity] = own[core]

    pl.semaphore_wait(barrier, greeted)

    def column_copy(stream, step, half):
        to_xh, to_pair = (xh, pair + step) if stream == UP else (1 - xh, pair - step)
        return pltpu.make_async_remote_copy(
            src_ref=own.at[half],
            dst_ref=kv.at[stream, pair, y, half, parity],
            send_sem=send_z.at[stream, step, half],
            recv_sem=recv_z.at[stream, pair, parity],
            device_id=at(to_xh, (2 * to_pair + core + NZ) % NZ, y, half),
            device_id_type=MESH,
        )

    def arrival(stream, source, source_parity):
        return pltpu.make_async_remote_copy(
            src_ref=own.at[0],
            dst_ref=kv.at[stream, source, y, core, source_parity],
            send_sem=send_z.at[stream, 0, 0],
            recv_sem=recv_z.at[stream, source, source_parity],
            device_id=sibling,
            device_id_type=MESH,
        )

    def part_of(index):
        return pl.ds(index * HEADS * HEAD_DIM, min(HEADS, GROUPS - index * HEADS) * HEAD_DIM)

    swapped = [(mask_hbm, mask_ref), (q_hbm, q_ref)]
    swapped += [
        (result.at[:, part_of(index)], attended.at[:, part_of(index)]) for index in range(PARTS)
    ]

    def swap_copy(index):
        source, target = swapped[index]
        return pltpu.make_async_remote_copy(
            src_ref=source,
            dst_ref=target,
            send_sem=swap_send.at[index],
            recv_sem=swap_recv.at[index],
            device_id=partner,
            device_id_type=MESH,
        )

    def local_copy(index):
        source, target = swapped[index]
        return pltpu.make_async_copy(source, target, in_sem.at[len(staged) + index])

    def y_copy(stream, source, column, target, side):
        return pltpu.make_async_remote_copy(
            src_ref=kv.at[stream, source, column, core],
            dst_ref=kv.at[stream, source, column, core],
            send_sem=send_y.at[stream, source, side],
            recv_sem=recv_y.at[stream, source, side],
            device_id=target,
            device_id_type=MESH,
        )

    def core_copy(stream, source, column, side, half):
        return pltpu.make_async_remote_copy(
            src_ref=kv.at[stream, source, column, half],
            dst_ref=kv.at[stream, source, column, half],
            send_sem=send_core.at[stream, source, side],
            recv_sem=recv_core.at[stream, source, side],
            device_id=sibling,
            device_id_type=MESH,
        )

    y_left = (y + NY - 1) % NY
    y_right = (y + 1) % NY
    y_far = (y + 2) % NY

    sides = ((right, y_left), (left, y_right), (opposite, y_far))
    columns = (y_left, y_right, y_far, y)

    def active(stream, step):
        if stream == UP:
            return (step >= 0) & (step <= pair), pair - step
        return (xh == 1) & (step >= 0) & (step < PAIRS - pair), pair + step

    def column_send(step, act):
        for half in range(2):

            @pl.when((xh == 0) & (step <= pair))
            def _():
                act(column_copy(DOWN, step, half))

            @pl.when((pair + step < PAIRS) & ((step > 0) | (core != parity) | (core != half)))
            def _():
                act(column_copy(UP, step, half))

    def forward(stream, step):
        on, source = active(stream, step)

        @pl.when(on)
        def _():
            for source_parity in range(2):
                if stream == UP:

                    @pl.when((step > 0) | (core != parity) | (core != source_parity))
                    def _():
                        arrival(stream, source, source_parity).wait_recv()
                else:
                    arrival(stream, source, source_parity).wait_recv()
            for side, (target, _) in enumerate(sides):
                y_copy(stream, source, y, target, side).start()
            core_copy(stream, source, y, 3, core).start()

    for step in range(WINDOW):
        column_send(step, lambda copy: copy.start())

    def share(stream, step):
        on, source = active(stream, step)

        @pl.when(on)
        def _():
            for side, (target, column) in enumerate(sides):
                y_copy(stream, source, column, target, side).wait_recv()
                core_copy(stream, source, column, side, core).start()

    def drain(stream, step):
        on, source = active(stream, step)

        @pl.when(on)
        def _():
            for side, (target, _) in enumerate(sides):
                y_copy(stream, source, y, target, side).wait_send()
            for side, column in enumerate(columns):
                core_copy(stream, source, column, side, core).wait_send()

    forward(UP, 0)
    forward(DOWN, 0)

    @pl.when(home)
    def _():
        for index in range(2):
            local_copy(index).start()

    @pl.when(core != parity)
    def _():
        for index in range(2):
            swap_copy(index).start()

    if WINDOW < PAIRS:
        column_send(WINDOW, lambda copy: copy.start())
    for part in range(NHEAD):
        weight_copy(part).start()

    for copy in stage[3:]:
        copy.wait()

    lanes = lax.broadcasted_iota(jnp.int32, (1, BLOCK), 1)
    places = query_seq * BLOCK + lanes
    doc_start = jnp.zeros((1, BLOCK), jnp.int32)
    end = doc_ref[0]
    for index in range(doc_ref.shape[0]):
        doc_start = jnp.where(places >= end, end, doc_start)
        if index + 1 < doc_ref.shape[0]:
            end = end + doc_ref[index + 1]
    own_turns = turn_ref[pl.ds(query_seq, 1), :]
    earlier = jnp.zeros((1, BLOCK), jnp.int32)
    for back in range(3):
        block = jnp.maximum(query_seq - back, 0)
        turns = turn_ref[pl.ds(block, 1), :].astype(jnp.float32)
        column = jnp.transpose(jnp.broadcast_to(turns, (BLOCK, BLOCK))).astype(jnp.int32)
        count = jnp.sum(jnp.where(column < own_turns, 1, 0), axis=0, keepdims=True)
        earlier = earlier + jnp.where(query_seq >= back, count, 0)
    turn_start = jnp.maximum(query_seq - 2, 0) * BLOCK + earlier

    def along_rows(row):
        wide = jnp.broadcast_to(row.astype(jnp.float32), (BLOCK, BLOCK))
        return jnp.transpose(wide).astype(jnp.int32)

    starts[0] = along_rows(doc_start)
    starts[1] = along_rows(turn_start)
    key_lanes = lax.broadcasted_iota(jnp.int32, (BLOCK, BLOCK), 1)
    mask_lanes = lax.broadcasted_iota(jnp.int32, mask_ref.shape, 1)
    query_places = query_seq * BLOCK + lax.broadcasted_iota(jnp.int32, (BLOCK, BLOCK), 0)

    best[...] = jnp.full_like(best, MASKED)
    summed[...] = jnp.zeros_like(summed)

    def divide(index, target):
        for group in range(index * HEADS, min((index + 1) * HEADS, GROUPS)):
            rows = slice(group * BLOCK, (group + 1) * BLOCK)
            target[:, group * HEAD_DIM : (group + 1) * HEAD_DIM] = (
                summed[rows, :HEAD_DIM] / summed[rows, HEAD_DIM:]
            ).astype(jnp.bfloat16)

    def attend(stream, step):
        on, source = active(stream, step)
        @pl.when(on)
        def _():
            for side, column in enumerate(columns):
                core_copy(stream, source, column, side, 1 - core).wait_recv()
            for index in range(2 * NY):
                block = (source * 2 + index // NY) * NY + index % NY
                if stream == UP:
                    block = block + xh * (NZ * NY)
                kept = jnp.sum(
                    jnp.where(mask_lanes == block, mask_ref[...], 0), axis=1, keepdims=True
                )
                same = jnp.where(block == query_seq, 1, 0)
                low = jnp.maximum(starts[0], starts[1] * (1 - jnp.maximum(kept, same)))
                places = block * BLOCK + key_lanes
                allowed = (places >= low) & (places <= query_places)
                bias[:, pl.ds(index * BLOCK, BLOCK)] = jnp.where(allowed, 0.0, MASKED)
            blocks = [(index % NY, index // NY) for index in range(2 * NY)]
            keys = jnp.concatenate([kv[stream, source, c, 0, r] for c, r in blocks], axis=0)
            values = jnp.concatenate([kv[stream, source, c, 1, r] for c, r in blocks], axis=0)
            values = jnp.concatenate([values, jnp.ones_like(values)], axis=1)
            for start in range(0, GROUPS, HEADS):
                heads = min(HEADS, GROUPS - start)
                rows = pl.ds(start * BLOCK, heads * BLOCK)
                scores = lax.dot_general(
                    q_rows[rows, :],
                    keys,
                    (((1,), (1,)), ((), ())),
                    preferred_element_type=jnp.float32,
                )
                scores = scores.reshape(heads, BLOCK, 2 * NY * BLOCK) + bias[...][None]
                scores = scores.reshape(heads * BLOCK, 2 * NY * BLOCK)
                previous = best[rows, :]
                newest = jnp.maximum(previous, jnp.max(scores, axis=1, keepdims=True))
                factor = jnp.exp2((previous - newest) * FACTOR)
                weights = jnp.exp2((scores - newest) * FACTOR)
                best[rows, :] = newest
                summed[rows, :] = summed[rows, :] * factor + jnp.dot(
                    weights.astype(jnp.bfloat16), values, preferred_element_type=jnp.float32
                )

    def take_queries():
        @pl.when(home)
        def _():
            for index in range(2):
                local_copy(index).wait()

        @pl.when(core != parity)
        def _():
            for index in range(2):
                swap_copy(index).wait_recv()

        for group in range(GROUPS):
            rows = slice(group * BLOCK, (group + 1) * BLOCK)
            q_rows[rows, :] = q_ref[:, group * HEAD_DIM : (group + 1) * HEAD_DIM]

    def advance(step, carry):
        @pl.when(step > 0)
        def _():
            forward(UP, step)
            forward(DOWN, step)
            if WINDOW < PAIRS:
                column_send(step + WINDOW, lambda copy: copy.start())

        @pl.when(step == ATTEND_LAG)
        def _():
            take_queries()

        attend(UP, step - ATTEND_LAG)
        attend(DOWN, step - ATTEND_LAG)
        share(UP, step - SHARE_LAG)
        share(DOWN, step - SHARE_LAG)
        return carry

    lax.fori_loop(0, PAIRS + ATTEND_LAG, advance, 0)

    @pl.when(home)
    def _():
        for index in range(PARTS):
            divide(index, attended)

    @pl.when(core != parity)
    def _():
        for index in range(PARTS):
            divide(index, result)
            swap_copy(2 + index).start()

    @pl.when(core != parity)
    def _():
        for index in range(PARTS):
            swap_copy(2 + index).wait_recv()

    for part in range(NHEAD):
        weight_copy(part).wait()

    def project(part, start, width):
        return jnp.dot(
            attended[...],
            w[part, :, pl.ds(start, width)],
            preferred_element_type=jnp.float32,
        )

    def sibling_copy(index):
        start, width = CHUNKS[index % len(CHUNKS)]
        place = index // len(CHUNKS)
        return pltpu.make_async_remote_copy(
            src_ref=rs_out.at[place, :, pl.ds(start, width)],
            dst_ref=rs_in.at[place, :, pl.ds(start, width)],
            send_sem=rs_send.at[index],
            recv_sem=rs_recv.at[index],
            device_id=sibling,
            device_id_type=MESH,
        )

    def cross_copy(index):
        start, width = CHUNKS[index]
        return pltpu.make_async_remote_copy(
            src_ref=cross_out.at[:, pl.ds(start, width)],
            dst_ref=cross_in.at[:, pl.ds(start, width)],
            send_sem=cross_send.at[index],
            recv_sem=cross_recv.at[index],
            device_id=across,
            device_id_type=MESH,
        )

    far = 1 - chip
    for index, (start, width) in enumerate(CHUNKS):
        rs_out[0, :, pl.ds(start, width)] = project(far * 2 + 1 - core, start, width).astype(
            jnp.bfloat16
        )
        sibling_copy(index).start()
    for index, (start, width) in enumerate(CHUNKS):
        mine = project(far * 2 + core, start, width)
        sibling_copy(index).wait_recv()
        cross_out[:, pl.ds(start, width)] = (
            mine + rs_in[0, :, pl.ds(start, width)].astype(jnp.float32)
        ).astype(jnp.bfloat16)
        cross_copy(index).start()
    for index, (start, width) in enumerate(CHUNKS):
        rs_out[1, :, pl.ds(start, width)] = project(chip * 2 + 1 - core, start, width).astype(
            jnp.bfloat16
        )
        sibling_copy(len(CHUNKS) + index).start()
    for index, (start, width) in enumerate(CHUNKS):
        mine = project(head, start, width)
        sibling_copy(len(CHUNKS) + index).wait_recv()
        mine = mine + rs_in[1, :, pl.ds(start, width)].astype(jnp.float32)
        cross_copy(index).wait_recv()
        out_ref[:, pl.ds(start, width)] = (
            mine + cross_in[:, pl.ds(start, width)].astype(jnp.float32)
        ).astype(jnp.bfloat16)

    for index in range(2 * len(CHUNKS)):
        sibling_copy(index).wait_send()
    for index in range(len(CHUNKS)):
        cross_copy(index).wait_send()

    def finish(step, carry):
        drain(UP, step)
        drain(DOWN, step)
        return carry

    lax.fori_loop(0, PAIRS, finish, 0)
    for step in range(PAIRS):
        column_send(step, lambda copy: copy.wait_send())

    @pl.when(core != parity)
    def _():
        for index in range(2 + PARTS):
            swap_copy(index).wait_send()


def on_device(
    queries, key_codes, value_codes, kv_scales, out_weight, turn_ids, block_mask, doc_lengths
):
    dma = pltpu.SemaphoreType.DMA
    return pl.pallas_call(
        kernel,
        out_shape=jax.ShapeDtypeStruct(queries.shape, jnp.bfloat16),
        in_specs=[pl.BlockSpec(memory_space=pltpu.HBM)] * 8,
        out_specs=pl.BlockSpec(memory_space=pltpu.VMEM),
        scratch_shapes=[
            pltpu.VMEM(queries.shape, jnp.bfloat16),
            pltpu.VMEM(key_codes.shape, jnp.bfloat16),
            pltpu.VMEM(value_codes.shape, jnp.bfloat16),
            pltpu.SMEM((2,), jnp.float32),
            pltpu.VMEM((turn_ids.shape[0] // BLOCK, BLOCK), jnp.int32),
            pltpu.VMEM(block_mask.shape, jnp.int32),
            pltpu.SMEM(doc_lengths.shape, jnp.int32),
            pltpu.VMEM((2, BLOCK, HEAD_DIM), jnp.bfloat16),
            pltpu.VMEM((2, PAIRS, NY, 2, 2, BLOCK, HEAD_DIM), jnp.bfloat16),
            pltpu.VMEM((GROUPS * BLOCK, HEAD_DIM), jnp.bfloat16),
            pltpu.VMEM((NHEAD, WIDTH, WIDTH), jnp.bfloat16),
            pltpu.VMEM((BLOCK, 2 * NY * BLOCK), jnp.float32),
            pltpu.VMEM((2, BLOCK, BLOCK), jnp.int32),
            pltpu.VMEM((GROUPS * BLOCK, 1), jnp.float32),
            pltpu.VMEM((GROUPS * BLOCK, 2 * HEAD_DIM), jnp.float32),
            pltpu.VMEM((BLOCK, WIDTH), jnp.bfloat16),
            pltpu.VMEM((BLOCK, WIDTH), jnp.bfloat16),
            pltpu.VMEM((2, BLOCK, WIDTH), jnp.bfloat16),
            pltpu.VMEM((2, BLOCK, WIDTH), jnp.bfloat16),
            pltpu.VMEM((BLOCK, WIDTH), jnp.bfloat16),
            pltpu.VMEM((BLOCK, WIDTH), jnp.bfloat16),
            dma((NHEAD,)),
            dma((7,)),
            dma((2, PAIRS, 2)),
            dma((2, PAIRS, 2)),
            dma((2, PAIRS, 3)),
            dma((2, PAIRS, 3)),
            dma((2, PAIRS, 4)),
            dma((2, PAIRS, 4)),
            dma((2 + PARTS,)),
            dma((2 + PARTS,)),
            dma((2 * len(CHUNKS),)),
            dma((2 * len(CHUNKS),)),
            dma((len(CHUNKS),)),
            dma((len(CHUNKS),)),
        ],
        compiler_params=pltpu.CompilerParams(
            collective_id=0, has_side_effects=True, vmem_limit_bytes=40 * 1024 * 1024
        ),
    )(
        *(
            pltpu.with_memory_space_constraint(operand, pltpu.HBM)
            for operand in (
                queries,
                key_codes,
                value_codes,
                kv_scales.reshape(2),
                out_weight,
                turn_ids.reshape(-1, BLOCK),
                block_mask,
                doc_lengths,
            )
        )
    )


def solution(mesh):
    placed = (
        P("seq", "head"),
        P("seq", "head"),
        P("seq", "head"),
        P(None, "seq", "head"),
        P("head", None),
        P(),
        P("seq", None),
        P(),
    )
    return jax.shard_map(
        on_device, mesh=mesh, in_specs=placed, out_specs=P("seq", "head"), check_vma=False
    )
```

time: 50.4 us -> 48 us (0.952)
  Pallas kernels: 49.4 us -> 47.1 us
    pallas_call x1, Pallas kernels: 49.4 us -> 47.1 us  [on_device(): pl.pallas_call(kernel, out_shape=jax.ShapeDtypeStruct(queries.shape, jnp....]
where the time goes in v4:
time: 48 us; the launch traced here: 47.8 us
  Pallas kernels  47.1 us (98%)
  local copies, waits for them, and re-layouts  0.69 us (1%)
    pallas_call x1, Pallas kernels, on_device(): pl.pallas_call(kernel, out_shape=jax.ShapeDtypeStruct(queries.shape, jnp....  47.1 us

profile of v4, /device:TPU:4, one launch (start us, length us, event | category | flops | bytes accessed | tf_op | source)
XLA Modules:
  0.0 47.8 jit_solution(11998859032432126627)
XLA Ops:
  0.0 47.1 %shard_map.82 = bf16[128,896]{1,0:T(8,128)(2,1)S(1)} custom-call(bf16[128,896]{1,0:T(8,128)(2,1)} %q_hbm.1, bf16[128,128]{1,0:T(8,128)(2,1)} %kc_hbm.1, bf16[128,128]{1,0:T(8,128)(2,1)} %vc_hbm.1, f32[2]{0:T(128)} %bitcast.3, bf16[896,3584]{1,0:T(8,128)(2,1)} %w_ref.1, s32[64,128]{1,0:T(8,128)} %bitcast.2, s32[1,64]{1,0:T(1,128)} %mask_hbm.1, s32[4]{0:T(128)} %doc_hbm.1), custom_call_target="tpu_custom_call" | custom-call | tf_op jit(solution)/shard_map/pallas_call | solution.py:507
  47.2 0.7 %copy.10 = bf16[128,896]{1,0:T(8,128)(2,1)} copy(bf16[128,896]{1,0:T(8,128)(2,1)S(1)} %shard_map.82) | data formatting | bytes 458752

commit v5 on v4

--- a/solution.py
+++ b/solution.py
@@ -242,8 +242,8 @@
                         arrival(stream, source, source_parity).wait_recv()
                 else:
                     arrival(stream, source, source_parity).wait_recv()
-            for side, (target, _) in enumerate(sides):
-                y_copy(stream, source, y, target, side).start()
+            for side in (2, 0, 1):
+                y_copy(stream, source, y, sides[side][0], side).start()
             core_copy(stream, source, y, 3, core).start()
 
     for step in range(WINDOW):
@@ -327,47 +327,64 @@
                 summed[rows, :HEAD_DIM] / summed[rows, HEAD_DIM:]
             ).astype(jnp.bfloat16)
 
+    def attend_pair(stream, source, leaving):
+        for side, column in enumerate(columns):
+            core_copy(stream, source, column, side, 1 - core).wait_recv()
+        for index in range(2 * NY):
+            block = (source * 2 + index // NY) * NY + index % NY
+            if stream == UP:
+                block = block + xh * (NZ * NY)
+            kept = jnp.sum(
+                jnp.where(mask_lanes == block, mask_ref[...], 0), axis=1, keepdims=True
+            )
+            same = jnp.where(block == query_seq, 1, 0)
+            low = jnp.maximum(starts[0], starts[1] * (1 - jnp.maximum(kept, same)))
+            places = block * BLOCK + key_lanes
+            allowed = (places >= low) & (places <= query_places)
+            bias[:, pl.ds(index * BLOCK, BLOCK)] = jnp.where(allowed, 0.0, MASKED)
+        blocks = [(index % NY, index // NY) for index in range(2 * NY)]
+        keys = jnp.concatenate([kv[stream, source, c, 0, r] for c, r in blocks], axis=0)
+        values = jnp.concatenate([kv[stream, source, c, 1, r] for c, r in blocks], axis=0)
+        values = jnp.concatenate([values, jnp.ones_like(values)], axis=1)
+        for start in range(0, GROUPS, HEADS):
+            heads = min(HEADS, GROUPS - start)
+            rows = pl.ds(start * BLOCK, heads * BLOCK)
+            scores = lax.dot_general(
+                q_rows[rows, :],
+                keys,
+                (((1,), (1,)), ((), ())),
+                preferred_element_type=jnp.float32,
+            )
+            scores = scores.reshape(heads, BLOCK, 2 * NY * BLOCK) + bias[...][None]
+            scores = scores.reshape(heads * BLOCK, 2 * NY * BLOCK)
+            previous = best[rows, :]
+            newest = jnp.maximum(previous, jnp.max(scores, axis=1, keepdims=True))
+            factor = jnp.exp2((previous - newest) * FACTOR)
+            weights = jnp.exp2((scores - newest) * FACTOR)
+            best[rows, :] = newest
+            summed[rows, :] = summed[rows, :] * factor + jnp.dot(
+                weights.astype(jnp.bfloat16), values, preferred_element_type=jnp.float32
+            )
+            if leaving:
+                divide(start // HEADS, result)
+                swap_copy(2 + start // HEADS).start()
+
     def attend(stream, step):
         on, source = active(stream, step)
-        @pl.when(on)
-        def _():
-            for side, column in enumerate(columns):
-                core_copy(stream, source, column, side, 1 - core).wait_recv()
-            for index in range(2 * NY):
-                block = (source * 2 + index // NY) * NY + index % NY
-                if stream == UP:
-                    block = block + xh * (NZ * NY)
-                kept = jnp.sum(
-                    jnp.where(mask_lanes == block, mask_ref[...], 0), axis=1, keepdims=True
-                )
-                same = jnp.where(block == query_seq, 1, 0)
-                low = jnp.maximum(starts[0], starts[1] * (1 - jnp.maximum(kept, same)))
-                places = block * BLOCK + key_lanes
-                allowed = (places >= low) & (places <= query_places)
-                bias[:, pl.ds(index * BLOCK, BLOCK)] = jnp.where(allowed, 0.0, MASKED)
-            blocks = [(index % NY, index // NY) for index in range(2 * NY)]
-            keys = jnp.concatenate([kv[stream, source, c, 0, r] for c, r in blocks], axis=0)
-            values = jnp.concatenate([kv[stream, source, c, 1, r] for c, r in blocks], axis=0)
-            values = jnp.concatenate([values, jnp.ones_like(values)], axis=1)
-            for start in range(0, GROUPS, HEADS):
-                heads = min(HEADS, GROUPS - start)
-                rows = pl.ds(start * BLOCK, heads * BLOCK)
-                scores = lax.dot_general(
-                    q_rows[rows, :],
-                    keys,
-                    (((1,), (1,)), ((), ())),
-                    preferred_element_type=jnp.float32,
-                )
-                scores = scores.reshape(heads, BLOCK, 2 * NY * BLOCK) + bias[...][None]
-                scores = scores.reshape(heads * BLOCK, 2 * NY * BLOCK)
-                previous = best[rows, :]
-                newest = jnp.maximum(previous, jnp.max(scores, axis=1, keepdims=True))
-                factor = jnp.exp2((previous - newest) * FACTOR)
-                weights = jnp.exp2((scores - newest) * FACTOR)
-                best[rows, :] = newest
-                summed[rows, :] = summed[rows, :] * factor + jnp.dot(
-                    weights.astype(jnp.bfloat16), values, preferred_element_type=jnp.float32
-                )
+        down_last = (xh == 1) & (PAIRS - 1 - pair >= pair)
+        if stream == UP:
+            last = (step == pair) & jnp.logical_not(down_last)
+        else:
+            last = (step == PAIRS - 1 - pair) & down_last
+        leaving = last & (core != parity)
+
+        @pl.when(on & jnp.logical_not(leaving))
+        def _():
+            attend_pair(stream, source, False)
+
+        @pl.when(on & leaving)
+        def _():
+            attend_pair(stream, source, True)
 
     def take_queries():
         @pl.when(home)
@@ -408,12 +425,6 @@
     def _():
         for index in range(PARTS):
             divide(index, attended)
-
-    @pl.when(core != parity)
-    def _():
-        for index in range(PARTS):
-            divide(index, result)
-            swap_copy(2 + index).start()
 
     @pl.when(core != parity)
     def _():

time: 48 us -> 47.7 us (level)
  no operation moved by 1% of the time
where the time goes in v5:
time: 47.7 us; the launch traced here: 47.5 us
  Pallas kernels  46.8 us (98%)
  local copies, waits for them, and re-layouts  0.69 us (1%)
    pallas_call x1, Pallas kernels, on_device(): pl.pallas_call(kernel, out_shape=jax.ShapeDtypeStruct(queries.shape, jnp....  46.8 us

profile of v5, /device:TPU:4, one launch (start us, length us, event | category | flops | bytes accessed | tf_op | source)
XLA Modules:
  0.0 47.5 jit_solution(3824069145239943618)
XLA Ops:
  0.0 46.8 %shard_map.82 = bf16[128,896]{1,0:T(8,128)(2,1)S(1)} custom-call(bf16[128,896]{1,0:T(8,128)(2,1)} %q_hbm.1, bf16[128,128]{1,0:T(8,128)(2,1)} %kc_hbm.1, bf16[128,128]{1,0:T(8,128)(2,1)} %vc_hbm.1, f32[2]{0:T(128)} %bitcast.3, bf16[896,3584]{1,0:T(8,128)(2,1)} %w_ref.1, s32[64,128]{1,0:T(8,128)} %bitcast.2, s32[1,64]{1,0:T(1,128)} %mask_hbm.1, s32[4]{0:T(128)} %doc_hbm.1), custom_call_target="tpu_custom_call" | custom-call | tf_op jit(solution)/shard_map/pallas_call | solution.py:518
  46.9 0.7 %copy.10 = bf16[128,896]{1,0:T(8,128)(2,1)} copy(bf16[128,896]{1,0:T(8,128)(2,1)S(1)} %shard_map.82) | data formatting | bytes 458752

commit v6 on v5

--- a/solution.py
+++ b/solution.py
@@ -270,6 +270,8 @@
 
     forward(UP, 0)
     forward(DOWN, 0)
+    if WINDOW < PAIRS:
+        column_send(WINDOW, lambda copy: copy.start())
 
     @pl.when(home)
     def _():
@@ -281,8 +283,6 @@
         for index in range(2):
             swap_copy(index).start()
 
-    if WINDOW < PAIRS:
-        column_send(WINDOW, lambda copy: copy.start())
     for part in range(NHEAD):
         weight_copy(part).start()
 

time: 47.7 us -> 47.7 us (level)
  no operation moved by 1% of the time
where the time goes in v6:
time: 47.7 us; the launch traced here: 47.5 us
  Pallas kernels  46.8 us (98%)
  local copies, waits for them, and re-layouts  0.69 us (1%)
    pallas_call x1, Pallas kernels, on_device(): pl.pallas_call(kernel, out_shape=jax.ShapeDtypeStruct(queries.shape, jnp....  46.8 us

profile of v6, /device:TPU:4, one launch (start us, length us, event | category | flops | bytes accessed | tf_op | source)
XLA Modules:
  0.0 47.5 jit_solution(16082786390379328576)
XLA Ops:
  0.0 46.8 %shard_map.82 = bf16[128,896]{1,0:T(8,128)(2,1)S(1)} custom-call(bf16[128,896]{1,0:T(8,128)(2,1)} %q_hbm.1, bf16[128,128]{1,0:T(8,128)(2,1)} %kc_hbm.1, bf16[128,128]{1,0:T(8,128)(2,1)} %vc_hbm.1, f32[2]{0:T(128)} %bitcast.3, bf16[896,3584]{1,0:T(8,128)(2,1)} %w_ref.1, s32[64,128]{1,0:T(8,128)} %bitcast.2, s32[1,64]{1,0:T(1,128)} %mask_hbm.1, s32[4]{0:T(128)} %doc_hbm.1), custom_call_target="tpu_custom_call" | custom-call | tf_op jit(solution)/shard_map/pallas_call | solution.py:518
  46.9 0.7 %copy.10 = bf16[128,896]{1,0:T(8,128)(2,1)} copy(bf16[128,896]{1,0:T(8,128)(2,1)S(1)} %shard_map.82) | data formatting | bytes 458752
